TPU v7x, 32 devices: a whole 2x2x4 slice. The times are simulated.
32 devices in a mesh: task: 2 (over x), batch: 16 (over z, y, core).
Axes of the slice: x: 2, y: 2, z: 4, core: 2. Of those that a mesh axis runs over, the one named last changes fastest.
Arguments:
- inputs: bfloat16 [2, 128, 256, 2048], P('task', 'batch')
- crop_cuts: int32 [2, 128, 2], P('task', 'batch'), may hold values from 2 to 13
- threshold: bfloat16 [2, 128, 256, 2048], P('task', 'batch'), may hold values from 0 to 1
- w_reduce: bfloat16 [2048, 512], replicated, may hold values from -0.125 to 0.125
- w_spatial: bfloat16 [9, 512, 512], replicated, may hold values from -0.09375 to 0.09375
- w_expand: bfloat16 [512, 2048], replicated, may hold values from -0.25 to 0.25
- w_heads: bfloat16 [2, 2048, 256], P('task'), may hold values from -0.125 to 0.125
- gain_one: float32 [512], replicated, may hold values from 0.1 to 1.9
- bias_one: float32 [512], replicated, may hold values from -3 to 3
- gain_two: float32 [512], replicated, may hold values from 0.1 to 1.9
- bias_two: float32 [512], replicated, may hold values from -3 to 3
- gain_three: float32 [2048], replicated, may hold values from 0.1 to 1.9
- bias_three: float32 [2048], replicated, may hold values from -3 to 3
- cotangent: bfloat16 [2, 2, 128, 256, 256], P('task', None, 'batch')
Outputs:
- heads: float32 [2, 2, 128, 256, 256], P('task', None, 'batch')
- grad_inputs: bfloat16 [2, 128, 256, 2048], P('task', 'batch')
- grad_reduce: float32 [2048, 512], replicated
- grad_spatial: float32 [9, 512, 512], replicated
- grad_expand: float32 [512, 2048], replicated
- grad_heads: float32 [2, 2048, 256], P('task')
- grad_gain_one: float32 [512], replicated
- grad_bias_one: float32 [512], replicated
- grad_gain_two: float32 [512], replicated
- grad_bias_two: float32 [512], replicated
- grad_gain_three: float32 [2048], replicated
- grad_bias_three: float32 [2048], replicated
Inputs may be any that keep to these rules, and one draw needn't show every extreme that they name: `crop_cuts`: each entry is a row cut followed by a column cut of its canvas.
All inputs are finite; a program needn't handle non-finite values.
Results may differ from a plain program's by a relative error of at most 0.014.
Values may be sent and summed in bfloat16 or wider, within the bound.
A program may use at most 384 MiB of HBM per device.

v0:
```python
import functools
import math

import jax
import jax.numpy as jnp
from jax import lax
from jax.experimental import pallas as pl
from jax.experimental.pallas import tpu as pltpu
from jax.sharding import PartitionSpec as P

SIDE = 16
EPS = 1e-05
FLOOR = 0.1
SOFT = 0.25
ROOT_HALF = 0.7071067811865476
DENSITY = 0.3989422804014327
LOG2E = 1.4426950408889634
ERF_P = 0.3275911
ERF_A = (0.254829592, -0.284496736, 1.421413741, -1.453152027, 1.061405429)
ROWS_ROWS = (((0,), (0,)), ((), ()))
COLS_COLS = (((1,), (1,)), ((), ()))
MESH = pl.DeviceIdType.MESH
LOW = 4
VMEM_BYTES = 62 * 2**20


AGENDA = {
    "start": ((0, 0), (1, 0),),
    "lane1": ((0, 1),),
    "lane2": ((1, 1),),
    "sp2": ((2, 0),),
    "sp3": ((0, 2),),
    "sp4": ((2, 1),),
    "sp5": ((3, 0),),
    "sp7": ((1, 2), (3, 1),),
    "sp8": ((4, 0),),
    "tap0": ((0, 3),),
    "tap1": ((4, 1),),
    "tap2": ((2, 2),),
    "tap4": ((1, 3),),
    "tap5": ((0, 4),),
    "tap6": ((3, 2),),
    "tap9": ((1, 4), (4, 2),),
    "tap10": ((2, 3),),
    "xch": ((0, 5), (1, 5), (3, 3), (4, 3),),
    "inner": ((0, 6), (2, 4),),
    "red1": ((1, 6), (5, 0),),
    "red2": ((3, 4), (5, 1),),
    "red3": ((6, 0),),
    "inp0": ((0, 7), (4, 4), (6, 1),),
    "inp2": ((0, 8), (2, 5),),
    "inp3": ((1, 7),),
    "inp5": ((1, 8), (3, 5), (5, 2),),
    "inp7": ((6, 2), (4, 5),),
    "tail": ((2, 6), (3, 6), (5, 3), (6, 3), (4, 6), (5, 4), (2, 7), (6, 4), (2, 8), (3, 7), (5, 5), (3, 8), (6, 5), (4, 7), (5, 6), (4, 8), (6, 6), (5, 7), (5, 8), (6, 7), (6, 8),),
}


class Reduction:
    def __init__(self, grid, work, result, core, first, second, last, done, send, recv, far_send, far_recv, local, wide):
        self.grid, self.work, self.result = grid, work, result
        self.room, self.done = (core, first, second, last), done
        self.send, self.recv, self.far_send, self.far_recv = send, recv, far_send, far_recv
        self.local = local
        self.wide = wide
        self.rows, self.cols = work.shape
        sizes = self.sizes(self.rows, self.cols, wide, grid.far)
        self.pieces = sizes[2][0] // sizes[3][0]
        self.mine = lax.rem(grid.high, self.pieces)

    @staticmethod
    def sizes(rows, cols, wide, far):
        if wide:
            core = (rows, cols // 2)
            first = (rows, cols // 8)
            second = (rows, cols // 16)
        else:
            core = (rows // 2, cols)
            first = (rows // 2, cols // 4)
            second = (rows // 4, cols // 4)
        pieces = max(n for n in range(1, far + 1) if far % n == 0 and second[0] % (8 * n) == 0)
        return core, first, second, (second[0] // pieces, second[1])

    @staticmethod
    def scratch(rows, cols, wide, far):
        core, first, second, last = Reduction.sizes(rows, cols, wide, far)
        return [
            pltpu.VMEM(core, jnp.bfloat16),
            pltpu.VMEM((2,) + first, jnp.bfloat16),
            pltpu.VMEM((2,) + second, jnp.bfloat16),
            pltpu.VMEM((2, far) + last, jnp.bfloat16),
            pltpu.VMEM((2,) + last, jnp.bfloat16),
            pltpu.SemaphoreType.DMA((10,)),
            pltpu.SemaphoreType.DMA((10,)),
            pltpu.SemaphoreType.DMA((4, far)),
            pltpu.SemaphoreType.DMA((4, far)),
            pltpu.SemaphoreType.DMA((2,)),
        ]

    def view(self, core, part=None, first=None, second=None, piece=None, done=False):
        sizes = self.sizes(self.rows, self.cols, self.wide, self.grid.far)
        row = col = 0
        shape = sizes[0]
        if self.wide:
            col = core * (self.cols // 2)
            if part is not None:
                col = col + part * (self.cols // 4) + first * (self.cols // 8)
                shape = sizes[1]
            if second is not None:
                col = col + second * (self.cols // 16)
                shape = sizes[2]
        else:
            row = core * (self.rows // 2)
            if part is not None:
                col = part * (self.cols // 2) + first * (self.cols // 4)
                shape = sizes[1]
            if second is not None:
                row = row + second * (self.rows // 4)
                shape = sizes[2]
        if piece is not None:
            row = row + piece * sizes[3][0]
            shape = sizes[3]
        if not isinstance(row, int):
            row = pl.multiple_of(row, shape[0] & -shape[0])
        if not isinstance(col, int):
            col = pl.multiple_of(col, 128)
        ref = self.result if done else self.work
        return ref.at[pl.ds(row, shape[0]), pl.ds(col, shape[1])]

    def swap(self, index):
        grid = self.grid
        part = (index + 1) % 2
        bits = grid.bits(part)
        if index == 0:
            source, target, device = self.view(1 - grid.core), self.room[0], grid.core_peer
        elif index < 3:
            source, target = self.view(grid.core, part, 1 - bits[0]), self.room[1].at[part]
            device = grid.peers(part)[0]
        elif index < 5:
            source, target = self.view(grid.core, part, bits[0], 1 - bits[1]), self.room[2].at[part]
            device = grid.peers(part)[1]
        elif index < 7:
            source = self.view(grid.core, part, bits[0], bits[1], done=True)
            target, device = source, grid.peers(part)[1]
        elif index < 9:
            source = self.view(grid.core, part, bits[0], done=True)
            target, device = source, grid.peers(part)[0]
        else:
            source = self.view(grid.core, done=True)
            target, device = source, grid.core_peer
        return pltpu.make_async_remote_copy(
            src_ref=source,
            dst_ref=target,
            send_sem=self.send.at[index],
            recv_sem=self.recv.at[index],
            device_id=device,
            device_id_type=MESH,
        )

    def add(self, target, sources):
        rows = target.shape[0]
        step = math.gcd(rows, 64)

        def one(i, carry):
            span = pl.ds(pl.multiple_of(i * step, step), step)
            total = sources[0][span].astype(jnp.float32)
            for source in sources[1:]:
                total = total + source[span].astype(jnp.float32)
            target[span] = total.astype(jnp.bfloat16)
            return carry

        lax.fori_loop(0, rows // step, one, 0)

    def join(self, mine, received):
        self.add(mine, [mine, received])

    def far_copy(self, part, step, back, inward):
        grid = self.grid
        bits = grid.bits(part)
        if back:
            first = grid.high - self.mine
            slot = first + lax.rem(self.mine + step, self.pieces)
            owner = slot if inward else grid.high
            source = self.done.at[part]
            target = self.view(grid.core, part, bits[0], bits[1], lax.rem(owner, self.pieces), True)
        else:
            slot = lax.rem(grid.high + step, grid.far)
            owner = slot if inward else grid.high
            source = self.view(grid.core, part, bits[0], bits[1], lax.rem(slot, self.pieces))
            target = self.room[3].at[part, owner]
        line = 2 * part + (1 if back else 0)
        return pltpu.make_async_remote_copy(
            src_ref=source,
            dst_ref=target,
            send_sem=self.far_send.at[line, step],
            recv_sem=self.far_recv.at[line, owner],
            device_id=(grid.task, slot * LOW + grid.low),
            device_id_type=MESH,
        )

    def far_start(self, back):
        for part in range(2):
            for step in range(1, self.pieces if back else self.grid.far):
                self.far_copy(part, step, back, False).start()

    def far_settle(self, back):
        for part in range(2):
            for step in range(1, self.pieces if back else self.grid.far):
                self.far_copy(part, step, back, True).wait_recv()
                self.far_copy(part, step, back, False).wait_send()

    def keep(self, part):
        bits = self.grid.bits(part)
        mine = self.view(self.grid.core, part, bits[0], bits[1], self.mine, True)
        return pltpu.make_async_copy(self.done.at[part], mine, self.local.at[part])

    def stage(self, index):
        grid = self.grid
        if index == 0:
            self.swap(0).start()
        elif index == 1:
            self.swap(0).wait()
            self.join(self.view(grid.core), self.room[0])
            for part in range(2):
                self.swap(1 + part).start()
        elif index == 2:
            for part in range(2):
                self.swap(1 + part).wait()
                bits = grid.bits(part)
                self.join(self.view(grid.core, part, bits[0]), self.room[1].at[part])
                self.swap(3 + part).start()
        elif index == 3:
            for part in range(2):
                self.swap(3 + part).wait()
                bits = grid.bits(part)
                self.join(self.view(grid.core, part, bits[0], bits[1]), self.room[2].at[part])
            self.far_start(False)
        elif index == 4:
            self.far_settle(False)
            for part in range(2):
                bits = grid.bits(part)
                mine = self.view(grid.core, part, bits[0], bits[1], self.mine)
                self.room[3][part, grid.high] = mine[...]
                self.add(self.done.at[part], [self.room[3].at[part, slot] for slot in range(grid.far)])
                self.keep(part).start()
            self.far_start(True)
        elif index == 5:
            self.far_settle(True)
            for part in range(2):
                self.keep(part).wait()
                self.swap(5 + part).start()
        elif index == 6:
            for part in range(2):
                self.swap(5 + part).wait()
                self.swap(7 + part).start()
        elif index == 7:
            for part in range(2):
                self.swap(7 + part).wait()
            self.swap(9).start()
        elif index == 8:
            self.swap(9).wait()


class Grid:
    def __init__(self, batch):
        self.task = lax.axis_index("task")
        place = lax.axis_index("batch")
        self.far = batch // LOW
        self.high = place // LOW
        self.low = lax.rem(place, LOW)
        self.core = lax.rem(place, 2)
        self.y = lax.rem(place // 2, 2)
        base = place - self.low
        self.core_peer = (self.task, base + self.y * 2 + (1 - self.core))
        self.x_peer = (1 - self.task, place)
        self.y_peer = (self.task, base + (1 - self.y) * 2 + self.core)

    def bits(self, part):
        return (self.task, self.y) if part == 0 else (self.y, self.task)

    def peers(self, part):
        return (self.x_peer, self.y_peer) if part == 0 else (self.y_peer, self.x_peer)


class Exchange:
    def __init__(self, tasks, batch, near, far, near_send, near_recv, far_send, far_recv):
        place = lax.axis_index("batch")
        self.task = lax.axis_index("task")
        self.high = place // LOW
        self.low = lax.rem(place, LOW)
        self.near_size = tasks * LOW
        self.far_size = batch // LOW
        self.me_near = self.task * LOW + self.low
        self.near, self.far = near, far
        self.near_sems, self.far_sems = (near_send, near_recv), (far_send, far_recv)

    @staticmethod
    def scratch(tasks, batch, width):
        near_size, far_size = tasks * LOW, batch // LOW
        return [
            pltpu.VMEM((near_size + 1, 2, width), jnp.float32),
            pltpu.VMEM((far_size + 1, 2, width), jnp.float32),
            pltpu.SemaphoreType.DMA((near_size,)),
            pltpu.SemaphoreType.DMA((near_size,)),
            pltpu.SemaphoreType.DMA((far_size,)),
            pltpu.SemaphoreType.DMA((far_size,)),
        ]

    def near_peer(self, step):
        slot = lax.rem(self.me_near + step, self.near_size)
        return slot, (slot // LOW, self.high * LOW + lax.rem(slot, LOW))

    def far_peer(self, step):
        slot = lax.rem(self.high + step, self.far_size)
        return slot, (self.task, slot * LOW + self.low)

    def peers(self):
        near = [self.near_peer(step)[1] for step in range(1, self.near_size)]
        return near + [self.far_peer(step)[1] for step in range(1, self.far_size)]

    def greet(self):
        barrier = pltpu.get_barrier_semaphore()
        for device in self.peers():
            pl.semaphore_signal(barrier, inc=1, device_id=device, device_id_type=MESH)

    def met(self):
        pl.semaphore_wait(pltpu.get_barrier_semaphore(), self.near_size + self.far_size - 2)

    def hop(self, size, peer, me, held, sems, filler=None):
        def copy(step, slot):
            return pltpu.make_async_remote_copy(
                src_ref=held.at[size],
                dst_ref=held.at[slot],
                send_sem=sems[0].at[step],
                recv_sem=sems[1].at[slot],
                device_id=peer(step)[1],
                device_id_type=MESH,
            )

        for step in range(1, size):
            copy(step, me).start()
        held[me] = held[size]
        if filler is not None:
            filler()
        for step in range(1, size):
            copy(step, peer(step)[0]).wait_recv()
        for step in range(1, size):
            copy(step, me).wait_send()
        return held[:size]

    def run(self, total, spread, rows, forward, fillers=(None, None)):
        self.near[self.near_size, 0:1] = total
        self.near[self.near_size, 1:2] = spread
        held = self.hop(self.near_size, self.near_peer, self.me_near, self.near, self.near_sems, fillers[0])
        total, spread = join(held, float(rows), forward)
        self.far[self.far_size, 0:1] = total
        self.far[self.far_size, 1:2] = spread
        held = self.hop(self.far_size, self.far_peer, self.high, self.far, self.far_sems, fillers[1])
        return join(held, float(rows * self.near_size), forward)


def join(held, share, forward):
    sums = held[:, 0, :]
    total = jnp.sum(sums, axis=0, keepdims=True)
    spread = jnp.sum(held[:, 1, :], axis=0, keepdims=True)
    if forward:
        groups = held.shape[0]
        away = sums * (1.0 / share) - total * (1.0 / (share * groups))
        spread = spread + share * jnp.sum(away * away, axis=0, keepdims=True)
    return total, spread


def settle_stats(exchange, stat_ref, vec_ref, out_ref, rows, count, forward, fillers=(None, None)):
    first = jnp.sum(stat_ref[:8], axis=0, keepdims=True)
    second = jnp.sum(stat_ref[8:16], axis=0, keepdims=True)
    out_ref[:8] = vec_ref[:8]
    if forward:
        local = first + rows * stat_ref[16:17]
        total, spread = exchange.run(local, second - first * first * (1.0 / rows), rows, True, fillers)
        scale = lax.rsqrt(spread * (1.0 / count) + EPS)
        out_ref[0:1] = total * (1.0 / count)
        out_ref[1:2] = scale
        out_ref[4:5] = scale * vec_ref[2:3]
        out_ref[8:] = jnp.zeros_like(out_ref[8:])
    else:
        total, spread = exchange.run(first, second, rows, False, fillers)
        out_ref[5:6] = total * (1.0 / count)
        out_ref[6:7] = spread * (1.0 / count)
        out_ref[8:9] = total
        out_ref[9:10] = spread
        out_ref[10:] = jnp.zeros_like(out_ref[10:])


def tail_and_bell(value):
    bell = jnp.exp2(value * value * (-0.5 * LOG2E))
    away = jnp.abs(value)
    ratio = 1.0 / (1.0 + away * (ERF_P * ROOT_HALF))
    poly = ERF_A[4]
    for factor in ERF_A[3::-1]:
        poly = poly * ratio + factor
    tail = 0.5 * poly * ratio * bell
    return jnp.where(value >= 0, 1.0 - tail, tail), bell


def fold(array):
    total = array[:8]
    for start in range(8, array.shape[0], 8):
        total = total + array[start : start + 8]
    return total


def crown_kernel(
    piece, h_ref, x_ref, thr_ref, cot_ref, cot_peer_ref, top_ref, top_peer_ref, vec_ref,
    out_ref, flow_ref, normed_ref, grad_ref, came_ref, stat_ref, z_ref, acc_ref, sent_ref, sems,
):
    step = pl.program_id(0)
    rows, width = x_ref.shape
    half = cot_ref.shape[1]
    task = lax.axis_index("task")
    last = pl.num_programs(0) - 1

    def send(index):
        span = pl.ds(pl.multiple_of(index * rows, rows), rows)
        return across(sent_ref.at[span], came_ref.at[span], sems.at[index])

    @pl.when(step > 0)
    def _():
        send(step - 1).start()

    @pl.when(step == 0)
    def _():
        stat_ref[...] = jnp.zeros_like(stat_ref)
        acc_ref[...] = jnp.zeros_like(acc_ref)

    for start in range(0, width, piece):
        cols = pl.ds(start, piece)
        g_one = lax.dot_general(
            cot_ref[...], top_ref[cols], COLS_COLS, preferred_element_type=jnp.float32
        ).astype(jnp.bfloat16).astype(jnp.float32)
        g_two = lax.dot_general(
            cot_peer_ref[...], top_peer_ref[cols], COLS_COLS, preferred_element_type=jnp.float32
        ).astype(jnp.bfloat16).astype(jnp.float32)
        total = g_one + g_two
        size = jnp.abs(g_one) + jnp.abs(g_two)
        share = total / jnp.maximum(size, FLOOR)
        limit = thr_ref[:, cols].astype(jnp.float32)
        keep = jnp.clip((0.5 / SOFT) * share + ((0.5 / SOFT + 0.5) - limit * (1.0 / SOFT)), 0.0, 1.0)
        merged = 0.5 * (total - size) + keep * size
        normed = (h_ref[:, cols] - vec_ref[0:1, cols]) * vec_ref[1:2, cols]
        normed_ref[:, cols] = normed.astype(jnp.bfloat16)
        before = normed * vec_ref[2:3, cols] + vec_ref[3:4, cols] + x_ref[:, cols].astype(jnp.float32)
        phi, bell = tail_and_bell(before)
        z_ref[:, cols] = (before * phi).astype(jnp.bfloat16)
        flow = merged * (phi + before * bell * DENSITY)
        flow_ref[:, cols] = flow.astype(flow_ref.dtype)
        stat_ref[:8, cols] += fold(flow)
        stat_ref[8:, cols] += fold(flow * normed)
    out_ref[...] = jnp.dot(z_ref[...], top_ref[...], preferred_element_type=jnp.float32)
    sent_ref[pl.ds(pl.multiple_of(step * rows, rows), rows)] = jnp.dot(
        z_ref[...], top_peer_ref[...], preferred_element_type=jnp.float32
    ).astype(jnp.bfloat16)
    acc_ref[:half] += lax.dot_general(cot_ref[...], z_ref[...], ROWS_ROWS, preferred_element_type=jnp.float32)
    acc_ref[half:] += lax.dot_general(cot_peer_ref[...], z_ref[...], ROWS_ROWS, preferred_element_type=jnp.float32)

    @pl.when(step == last)
    def _():
        mine = pl.multiple_of(task * half, half)
        peer = pl.multiple_of((1 - task) * half, half)
        grad_ref[:, pl.ds(mine, half)] = acc_ref[:half].T.astype(jnp.bfloat16)
        grad_ref[:, pl.ds(peer, half)] = acc_ref[half:].T.astype(jnp.bfloat16)
        send(last).start()

    def after():
        lax.fori_loop(0, last + 1, lambda index, carry: (send(index).wait(), carry)[1], 0)

    return after


def wide(mask, width):
    return jnp.concatenate([mask] * (width // mask.shape[1]), axis=1)


def gather_stats(stat_ref, hidden, first):
    @pl.when(first)
    def _():
        stat_ref[:16] = jnp.zeros_like(stat_ref[:16])
        mean = jnp.sum(hidden, axis=0, keepdims=True) / hidden.shape[0]
        stat_ref[16:] = jnp.broadcast_to(mean, stat_ref[16:].shape)

    away = hidden - stat_ref[16:17]
    stat_ref[:8] += fold(away)
    stat_ref[8:16] += fold(away * away)


def normal(hidden, vec_ref):
    return (hidden - vec_ref[0:1]) * vec_ref[1:2]


def squeeze_kernel(x_ref, w_ref, out_ref, stat_ref):
    hidden = jnp.dot(x_ref[...], w_ref[...], preferred_element_type=jnp.float32)
    out_ref[...] = hidden
    gather_stats(stat_ref, hidden, pl.program_id(0) == 0)


def mesh_kernel(h_ref, vec_ref, mask_ref, w_ref, out_ref, side_ref, stat_ref, pad_ref):
    rows, mid = h_ref.shape
    inner = pl.ds(SIDE, rows)
    before = normal(h_ref[...], vec_ref) * vec_ref[2:3] + vec_ref[3:4]
    phi, _ = tail_and_bell(before)
    low = (before * phi).astype(jnp.bfloat16)
    kept = low.astype(jnp.float32)
    left = wide(mask_ref[:, :128].astype(jnp.float32), mid)
    right = wide(mask_ref[:, 128:256].astype(jnp.float32), mid)

    @pl.when(pl.program_id(0) == 0)
    def _():
        pad_ref[:SIDE] = jnp.zeros_like(pad_ref[:SIDE])
        pad_ref[SIDE + rows :] = jnp.zeros_like(pad_ref[:SIDE])

    pad_ref[inner, :mid] = (pltpu.roll(kept, 1, 0) * left).astype(jnp.bfloat16)
    pad_ref[inner, mid : 2 * mid] = low
    pad_ref[inner, 2 * mid :] = (pltpu.roll(kept, rows - 1, 0) * right).astype(jnp.bfloat16)
    side_ref[...] = pad_ref[inner].T
    above = wide(mask_ref[:, 256:384], 3 * mid)
    below = wide(mask_ref[:, 384:], 3 * mid)
    hidden = jnp.dot(pad_ref[inner], w_ref[3 * mid : 6 * mid], preferred_element_type=jnp.float32)
    hidden += jnp.dot(pad_ref[:rows] * above, w_ref[: 3 * mid], preferred_element_type=jnp.float32)
    hidden += jnp.dot(pad_ref[2 * SIDE :] * below, w_ref[6 * mid :], preferred_element_type=jnp.float32)
    out_ref[...] = hidden
    gather_stats(stat_ref, hidden, pl.program_id(0) == 0)


def widen_kernel(h_ref, vec_ref, w_ref, out_ref, low_ref, stat_ref):
    before = normal(h_ref[...], vec_ref) * vec_ref[2:3] + vec_ref[3:4]
    phi, _ = tail_and_bell(before)
    low = (before * phi).astype(jnp.bfloat16)
    low_ref[...] = low.T
    hidden = jnp.dot(low, w_ref[...], preferred_element_type=jnp.float32)
    out_ref[...] = hidden
    gather_stats(stat_ref, hidden, pl.program_id(0) == 0)


def norm_grad(upstream, normed, vec_ref):
    return vec_ref[4:5] * (upstream - vec_ref[5:6] - normed * vec_ref[6:7])


def act_slope(value):
    phi, bell = tail_and_bell(value)
    return phi + value * bell * DENSITY


def gather_flow(stat_ref, flow, normed, first):
    @pl.when(first)
    def _():
        stat_ref[...] = jnp.zeros_like(stat_ref)

    stat_ref[:8] += fold(flow)
    stat_ref[8:16] += fold(flow * normed)


def narrow_kernel(flow_ref, normed_ref, vec_ref, two_ref, vectwo_ref, low_ref, w_ref, out_ref, grad_ref, stat_ref, dh_ref):
    step = pl.program_id(0)
    rows = flow_ref.shape[0]
    dh = norm_grad(flow_ref[...].astype(jnp.float32), normed_ref[...].astype(jnp.float32), vec_ref)
    low = dh.astype(jnp.bfloat16)
    dh_ref[pl.ds(pl.multiple_of(step * rows, rows), rows)] = low
    dq = lax.dot_general(low, w_ref[...], COLS_COLS, preferred_element_type=jnp.float32)
    normed = normal(two_ref[...], vectwo_ref)
    flow = dq * act_slope(normed * vectwo_ref[2:3] + vectwo_ref[3:4])
    out_ref[...] = flow
    gather_flow(stat_ref, flow, normed, step == 0)


def narrow_fill(flow_ref, normed_ref, vec_ref, two_ref, vectwo_ref, low_ref, w_ref, out_ref, grad_ref, stat_ref, dh_ref):
    half = dh_ref.shape[1] // 2

    def part(index):
        def run():
            def one(i, carry):
                cols = pl.ds(pl.multiple_of(index * half + i * 512, 512), 512)
                grad_ref[:, cols] = jnp.dot(
                    low_ref[...], dh_ref[:, cols], preferred_element_type=jnp.float32
                ).astype(jnp.bfloat16)
                return carry

            lax.fori_loop(0, half // 512, one, 0)

        return run

    return part(0), part(1)


def across(source, target, sems):
    return pltpu.make_async_remote_copy(
        src_ref=source,
        dst_ref=target,
        send_sem=sems.at[0],
        recv_sem=sems.at[1],
        device_id=(1 - lax.axis_index("task"), lax.axis_index("batch")),
        device_id_type=MESH,
    )


def tiled(kernel, tile, moving, flags, outs, fixed, scratch, name, stats=None, send=None, far=(), fill=None, turns=()):
    tasks = lax.axis_size("task")
    batch = lax.axis_size("batch")
    rows = moving[0].shape[0]

    def block(array):
        return pl.BlockSpec((tile,) + array.shape[1:], lambda i: (i,) + (0,) * (len(array.shape) - 1))

    def turned(array):
        return pl.BlockSpec((array.shape[0], tile), lambda i: (0, i))

    def whole(array):
        zeros = (0,) * len(array.shape)
        return pl.BlockSpec(array.shape, lambda i: zeros)

    hbm = pl.BlockSpec(memory_space=pl.ANY)
    operands = list(moving)
    in_specs = [block(a) if m else whole(a) for a, m in zip(moving, flags)]
    out_shape = outs + fixed + list(far)
    out_specs = [turned(a) if i in turns else block(a) for i, a in enumerate(outs)] + [whole(a) for a in fixed] + [hbm for a in far]
    scratch = list(scratch)
    params = dict(vmem_limit_bytes=VMEM_BYTES)
    ins, made, held = len(operands), len(out_shape), len(scratch)
    run = kernel
    if stats is not None:
        vec, forward, ident = stats
        width = vec.shape[1]
        params.update(collective_id=ident, has_side_effects=True)
        operands.append(vec)
        in_specs.append(whole(vec))
        out_shape = out_shape + [shape32(16, width)]
        out_specs = out_specs + [whole(out_shape[-1])]
        scratch = scratch + [pltpu.VMEM((24 if forward else 16, width), jnp.float32)]
        scratch = scratch + Exchange.scratch(tasks, batch, width)
        if send is not None:
            operands.append(send)
            in_specs.append(hbm)
            out_shape = out_shape + [jax.ShapeDtypeStruct(send.shape, send.dtype)]
            out_specs = out_specs + [hbm]
            scratch = scratch + [pltpu.SemaphoreType.DMA((2,))]

        def run(*refs):
            refs = list(refs)
            take = lambda n: [refs.pop(0) for _ in range(n)]
            used = take(ins)
            vec_ref = take(1)[0]
            source = take(1)[0] if send is not None else None
            given = take(made)
            out_ref = take(1)[0]
            target = take(1)[0] if send is not None else None
            own = take(held)
            stat_ref = take(1)[0]
            exchange = Exchange(tasks, batch, *take(6))
            step = pl.program_id(0)
            last = pl.num_programs(0) - 1

            @pl.when(step == 0)
            def _():
                exchange.greet()

            early = send is not None or len(far) > 0
            if early:

                @pl.when(step == 1)
                def _():
                    exchange.met()
                    if send is not None:
                        across(source, target, refs[0]).start()

            after = kernel(*used, *given, stat_ref, *own)

            @pl.when(step == last)
            def _():
                if not early:
                    exchange.met()
                fillers = (None, None) if fill is None else fill(*used, *given, stat_ref, *own)
                settle_stats(exchange, stat_ref, vec_ref, out_ref, rows, rows * tasks * batch, forward, fillers)
                if send is not None:
                    across(source, target, refs[0]).wait()
                if after is not None:
                    after()

    return pl.pallas_call(
        run,
        grid=(rows // tile,),
        out_shape=out_shape,
        in_specs=in_specs,
        out_specs=out_specs,
        scratch_shapes=scratch,
        compiler_params=pltpu.CompilerParams(**params),
        name=name,
    )(*operands)


def shape32(*shape):
    return jax.ShapeDtypeStruct(shape, jnp.float32)


def shape16(*shape):
    return jax.ShapeDtypeStruct(shape, jnp.bfloat16)


def squeeze(flat_in, w_reduce, stats, tile):
    rows, mid = flat_in.shape[0], w_reduce.shape[1]
    return tiled(squeeze_kernel, tile, [flat_in, w_reduce], [1, 0], [shape32(rows, mid)], [], [], "squeeze", stats)


def mesh_forward(h_one, vec, masks, taps, stats, send, tile):
    rows, mid = h_one.shape
    return tiled(
        mesh_kernel, tile, [h_one, vec, masks, taps], [1, 0, 1, 0],
        [shape32(rows, mid), shape16(3 * mid, rows)], [],
        [pltpu.VMEM((tile + 2 * SIDE, 3 * mid), jnp.bfloat16)], "mesh_forward", stats, send, turns=(1,),
    )


def widen(h_two, vec, w_expand, stats, send, tile):
    rows, mid = h_two.shape
    width = w_expand.shape[1]
    return tiled(
        widen_kernel, tile, [h_two, vec, w_expand], [1, 0, 0],
        [shape32(rows, width), shape16(mid, rows)], [], [], "widen", stats, send, turns=(1,),
    )


def narrow(flow, normed, vec_three, h_two, vec_two, q_two, w_expand, stats, tile):
    rows, mid = h_two.shape
    width = w_expand.shape[1]
    return tiled(
        narrow_kernel, tile, [flow, normed, vec_three, h_two, vec_two, q_two, w_expand], [1, 1, 0, 1, 0, 0, 0],
        [shape32(rows, mid)], [shape16(mid, width)], [pltpu.VMEM((rows, width), jnp.bfloat16)], "narrow", stats,
        fill=narrow_fill,
    )


def crown(h_three, flat_in, limits, cot, cot_peer, top, top_peer, vec, stats, tile, piece):
    rows, width = flat_in.shape
    half = cot.shape[1]
    return tiled(
        functools.partial(crown_kernel, piece), tile,
        [h_three, flat_in, limits, cot, cot_peer, top, top_peer, vec], [1, 1, 1, 1, 1, 0, 0, 0],
        [shape32(rows, half), shape16(rows, width), shape16(rows, width)], [shape16(width, 2 * half)],
        [
            pltpu.VMEM((tile, width), jnp.bfloat16),
            pltpu.VMEM((2 * half, width), jnp.float32),
            pltpu.VMEM((rows, half), jnp.bfloat16),
            pltpu.SemaphoreType.DMA((rows // tile, 2)),
        ],
        "crown", stats, None, [shape16(rows, half)],
    )


class Stream:
    def __init__(self, view, held, sems):
        self.view, self.held, self.sems = view, held, sems

    def copy(self, index):
        slot = lax.rem(index, 2)
        return pltpu.make_async_copy(self.view(index), self.held.at[slot], self.sems.at[slot])

    def start(self, index):
        self.copy(index).start()

    def take(self, index, count):
        self.copy(index).wait()

        @pl.when(index + 1 < count)
        def _():
            self.start(index + 1)

        return self.held.at[lax.rem(index, 2)]


def back_kernel(rows, tasks, batch, tile, *refs):
    refs = list(refs)

    def take(count):
        return [refs.pop(0) for _ in range(count)]

    (flow_hbm, two_hbm, one_hbm, side_hbm, mask_hbm, w_hbm, x_hbm, up_hbm, top_hbm, heads_hbm, expand_hbm) = take(11)
    vectwo_ref, vecone_ref = take(2)
    (out_hbm, heads_out, expand_out, spatial_out, reduce_out, vec_ref) = take(6)
    (two_buf, mask_buf, x_buf, up_buf, out_buf) = take(5)
    (side_ref, lane_ref, flow_ref, w_ref, top_ref) = take(5)
    small = up_buf.shape[1]
    heads_work, expand_work, spatial_work, reduce_work, stat_ref = take(5)
    pair_sems, whole_sems, flow_sems = take(3)
    exchange = Exchange(tasks, batch, *take(6))
    grid = Grid(batch)
    mid = flow_hbm.shape[1]
    width = x_hbm.shape[1]
    spans = rows // tile

    def blocks(ref, height):
        return lambda index: ref.at[pl.ds(pl.multiple_of(index * height, height), height)]

    exchange.greet()

    def flow_load(index):
        return pltpu.make_async_copy(
            blocks(flow_hbm, tile)(index), blocks(flow_ref, tile)(index), flow_sems.at[index]
        )

    twos = Stream(blocks(two_hbm, tile), two_buf, pair_sems.at[1])
    masks = Stream(blocks(mask_hbm, tile), mask_buf, pair_sems.at[2])
    ones = Stream(blocks(one_hbm, tile), two_buf, pair_sems.at[3])
    ups = Stream(blocks(up_hbm, small), up_buf, pair_sems.at[4])
    dh_ref, normed_ref, dht_ref = lane_ref.at[:, :mid], lane_ref.at[:, mid : 2 * mid], side_ref.at[:mid]
    across_cols = x_buf.shape[2]
    columns = Stream(
        lambda index: x_hbm.at[:, pl.ds(pl.multiple_of(index * across_cols, across_cols), across_cols)],
        x_buf, pair_sems.at[5],
    )
    loads = [
        pltpu.make_async_copy(source, target, whole_sems.at[index])
        for index, (source, target) in enumerate(
            [(heads_hbm, heads_work), (side_hbm, side_ref), (expand_hbm, expand_work), (w_hbm, w_ref), (top_hbm, top_ref)]
        )
    ]
    heads_load, side_load, expand_load, w_load, top_load = loads
    heads_load.start()
    for stream in (twos, masks):
        stream.start(0)
    for index in range(spans):
        flow_load(index).start()
    for load in loads[1:]:
        load.start()

    third = spatial_work.shape[0] // 3
    works = [(heads_work, heads_out, False), (expand_work, expand_out, True)]
    for index in range(3):
        span = pl.ds(index * third, third)
        works.append((spatial_work.at[span], spatial_out.at[span], False))
    for index in range(2):
        span = pl.ds(index * width // 2, width // 2)
        works.append((reduce_work.at[span], reduce_out.at[span], False))
    reductions = [Reduction(grid, work, out, *take(10), wide) for work, out, wide in works]

    def tick(name):
        for item, stage in AGENDA.get(name, ()):
            reductions[item].stage(stage)

    def ticks(name, index, count, scale=1, shift=0):
        for step in range(count):
            label = "%s%d" % (name, step * scale + shift)
            if label in AGENDA:

                @pl.when(index == step)
                def _():
                    tick(label)

    def lanes(index, carry):
        span = pl.ds(pl.multiple_of(index * tile, tile), tile)
        flow_load(index).wait()
        flow = flow_ref[span]
        normed = normal(twos.take(index, spans)[...], vectwo_ref)
        mask = masks.take(index, spans)
        dh = norm_grad(flow, normed, vectwo_ref)
        above = wide(mask[:, 256:384].astype(jnp.float32), mid)
        below = wide(mask[:, 384:].astype(jnp.float32), mid)
        low = jnp.bfloat16
        zero = jnp.zeros((SIDE, mid), low)
        lane_ref[span, mid : 2 * mid] = dh.astype(low)
        lane_ref[span, :mid] = jnp.concatenate([(dh * above)[SIDE:].astype(low), zero], axis=0)
        lane_ref[span, 2 * mid :] = jnp.concatenate([zero, (dh * below)[: tile - SIDE].astype(low)], axis=0)
        ticks("lane", index, 4)
        return carry

    exchange.met()
    heads_load.wait()
    expand_load.wait()
    tick("start")
    lax.fori_loop(0, spans, lanes, 0)
    masks.start(0)
    ones.start(0)
    side_load.wait()

    def spatial(index, carry):
        a, b = index // 3, lax.rem(index, 3)
        rows_here = pl.ds(pl.multiple_of(b * mid, mid), mid)
        cols = pl.ds(pl.multiple_of(a * mid, mid), mid)
        part = jnp.dot(side_ref[rows_here], lane_ref[:, cols], preferred_element_type=jnp.float32)
        spatial_work[pl.ds(pl.multiple_of(index * mid, mid), mid)] = part.astype(jnp.bfloat16)
        ticks("sp", index, 9)
        return carry

    lax.fori_loop(0, 9, spatial, 0)
    w_load.wait()

    def taps(index, carry):
        span = pl.ds(pl.multiple_of(index * tile, tile), tile)
        mask = masks.take(index, spans)
        pieces = []
        for b in range(3):
            total = None
            for a in range(3):
                part = lax.dot_general(
                    lane_ref[span, a * mid : (a + 1) * mid], w_ref[3 * a + b], COLS_COLS,
                    preferred_element_type=jnp.float32,
                )
                total = part if total is None else total + part
            pieces.append(total)
            if b < 2:
                ticks("tap", index, 4, 3, b)
        left = wide(mask[:, :128].astype(jnp.float32), mid)
        right = wide(mask[:, 128:256].astype(jnp.float32), mid)
        dq = pieces[1] + pltpu.roll(pieces[0] * left, tile - 1, 0) + pltpu.roll(pieces[2] * right, 1, 0)
        normed = normal(ones.take(index, spans)[...], vecone_ref)
        flow = dq * act_slope(normed * vecone_ref[2:3] + vecone_ref[3:4])
        flow_ref[span] = flow
        normed_ref[span] = normed.astype(jnp.bfloat16)
        gather_flow(stat_ref, flow, normed, index == 0)
        ticks("tap", index, 4, 3, 2)
        return carry

    lax.fori_loop(0, spans, taps, 0)
    columns.start(0)
    ups.start(0)
    settle_stats(exchange, stat_ref, vecone_ref, vec_ref, rows, rows * tasks * batch, False)
    tick("xch")

    def inner(index, carry):
        span = pl.ds(pl.multiple_of(index * tile, tile), tile)
        dh = norm_grad(flow_ref[span], normed_ref[span].astype(jnp.float32), vec_ref)
        dh_ref[span] = dh.astype(jnp.bfloat16)
        dht_ref[:, span] = dh.T.astype(jnp.bfloat16)
        return carry

    lax.fori_loop(0, spans, inner, 0)
    tick("inner")
    count = width // across_cols

    def reduce(index, carry):
        part = jnp.dot(dht_ref[...], columns.take(index, count)[...], preferred_element_type=jnp.float32)
        span = pl.ds(pl.multiple_of(index * across_cols, across_cols), across_cols)
        reduce_work[span] = part.T.astype(jnp.bfloat16)
        ticks("red", index, 4)
        return carry

    lax.fori_loop(0, count, reduce, 0)
    top_load.wait()

    def store(index):
        slot = lax.rem(index, 2)
        return pltpu.make_async_copy(out_buf.at[slot], blocks(out_hbm, small)(index), pair_sems.at[6, slot])

    def inputs(index, carry):
        span = pl.ds(pl.multiple_of(index * small, small), small)
        up = ups.take(index, rows // small)

        @pl.when(index >= 2)
        def _():
            store(index - 2).wait()

        slot = lax.rem(index, 2)
        for start in range(0, width, across_cols):
            cols = pl.ds(start, across_cols)
            part = lax.dot_general(dh_ref[span], top_ref[cols], COLS_COLS, preferred_element_type=jnp.float32)
            out_buf[slot, :, cols] = (up[:, cols].astype(jnp.float32) + part).astype(jnp.bfloat16)
        store(index).start()
        ticks("inp", index, 8)
        return carry

    lax.fori_loop(0, rows // small, inputs, 0)
    for index in range(rows // small - 2, rows // small):
        store(index).wait()
    tick("tail")


def back(flow, h_two, vec_two, h_one, vec_one, sides, masks, w_spatial, flat_in, up, w_reduce, heads, expand, ident, tile):
    tasks = lax.axis_size("task")
    batch = lax.axis_size("batch")
    far = batch // LOW
    rows, mid = h_one.shape
    width = flat_in.shape[1]
    full, low = jnp.float32, jnp.bfloat16
    cols = 512
    hbm = pl.BlockSpec(memory_space=pl.ANY)
    vmem = pl.BlockSpec(memory_space=pltpu.VMEM)
    shapes = [(heads.shape, False), (expand.shape, True)] + [((3 * mid, mid), False)] * 3
    shapes += [((width // 2, mid), False)] * 2
    scratch = [
        pltpu.VMEM((2, tile, mid), full),
        pltpu.VMEM((2, tile, 512), low),
        pltpu.VMEM((2, rows, cols), low),
        pltpu.VMEM((2, 256, width), low),
        pltpu.VMEM((2, 256, width), low),
        pltpu.VMEM((3 * mid, rows), low),
        pltpu.VMEM((rows, 3 * mid), low),
        pltpu.VMEM((rows, mid), full),
        pltpu.VMEM(w_spatial.shape, low),
        pltpu.VMEM(w_reduce.shape, low),
        pltpu.VMEM(heads.shape, low),
        pltpu.VMEM(expand.shape, low),
        pltpu.VMEM((9 * mid, mid), low),
        pltpu.VMEM((width, mid), low),
        pltpu.VMEM((16, mid), full),
        pltpu.SemaphoreType.DMA((7, 2)),
        pltpu.SemaphoreType.DMA((5,)),
        pltpu.SemaphoreType.DMA((rows // tile,)),
    ] + Exchange.scratch(tasks, batch, mid)
    for (high, across_), is_wide in shapes:
        scratch += Reduction.scratch(high, across_, is_wide, far)
    return pl.pallas_call(
        functools.partial(back_kernel, rows, tasks, batch, tile),
        out_shape=[
            shape16(rows, width), shape16(*heads.shape), shape16(*expand.shape), shape16(9 * mid, mid),
            shape16(width, mid), shape32(16, mid),
        ],
        in_specs=[hbm] * 11 + [vmem] * 2,
        out_specs=[hbm] * 5 + [vmem],
        scratch_shapes=scratch,
        compiler_params=pltpu.CompilerParams(
            vmem_limit_bytes=VMEM_BYTES, collective_id=ident, has_side_effects=True
        ),
        name="back",
    )(flow, h_two, h_one, sides, masks, w_spatial, flat_in, up, w_reduce, heads, expand, vec_two, vec_one)


def body(
    inputs,
    crop_cuts,
    threshold,
    w_reduce,
    w_spatial,
    w_expand,
    w_heads,
    gain_one,
    bias_one,
    gain_two,
    bias_two,
    gain_three,
    bias_three,
    cotangent,
):
    low = jnp.bfloat16
    full = jnp.float32
    canvases, pixels, width = inputs.shape[1:]
    mid = w_reduce.shape[1]
    rows = canvases * pixels
    half = w_heads.shape[2]
    task = lax.axis_index("task")
    cot = cotangent.reshape(2, rows, half)
    cot_mine = lax.dynamic_index_in_dim(cot, task, 0, keepdims=False)
    cot_sent = lax.dynamic_index_in_dim(cot, 1 - task, 0, keepdims=False)
    top_mine = w_heads[0]

    def params(gain, bias):
        zero = jnp.zeros_like(gain)
        return jnp.stack([zero, zero, gain, bias, zero, zero, zero, zero])

    lines = jnp.arange(SIDE, dtype=jnp.int32)
    cuts = crop_cuts.reshape(canvases, 2)
    from_above = jnp.logical_not((lines == cuts[:, 0:1]) | (lines == 0)[None, :])
    from_left = jnp.logical_not((lines == cuts[:, 1:2]) | (lines == 0)[None, :])
    from_below = jnp.pad(from_above[:, 1:], ((0, 0), (0, 1)))
    from_right = jnp.pad(from_left[:, 1:], ((0, 0), (0, 1)))
    shape = (canvases, SIDE, SIDE, 128)
    masks = jnp.concatenate(
        [jnp.broadcast_to(m[:, None, :, None], shape) for m in (from_left, from_right)]
        + [jnp.broadcast_to(m[:, :, None, None], shape) for m in (from_above, from_below)],
        axis=3,
    ).astype(low).reshape(rows, 512)

    flat_in = inputs.reshape(rows, width)
    h_one, vec_one = squeeze(flat_in, w_reduce, (params(gain_one, bias_one), True, 0), min(rows, 512))
    h_two, sides, vec_two, cot_peer = mesh_forward(
        h_one, vec_one, masks, w_spatial.reshape(9 * mid, mid), (params(gain_two, bias_two), True, 1), cot_sent, pixels
    )
    h_three, q_two, vec_three, top_peer = widen(
        h_two, vec_two, w_expand, (params(gain_three, bias_three), True, 2), top_mine, pixels
    )
    out_mine, flow, normed, grad_heads, out_peer, vec_three = crown(
        h_three, flat_in, threshold.reshape(rows, width), cot_mine, cot_peer, top_mine, top_peer, vec_three,
        (vec_three, False, 3), pixels, 256,
    )
    out_peer = out_peer.astype(full)
    first = jnp.where(task == 0, out_mine, out_peer)
    second = jnp.where(task == 0, out_peer, out_mine)
    head_out = jnp.stack([first, second]).reshape(1, 2, canvases, pixels, half)
    flow_two, grad_expand, vec_two = narrow(
        flow, normed, vec_three, h_two, vec_two, q_two, w_expand, (vec_two, False, 4), min(rows, 512)
    )
    grad_inputs, grad_heads, grad_expand, grad_spatial, grad_reduce, vec_one = back(
        flow_two, h_two, vec_two, h_one, vec_one, sides, masks, w_spatial, flat_in, flow, w_reduce,
        grad_heads, grad_expand, 5, min(rows, 512),
    )
    grad_heads = lax.dynamic_slice_in_dim(grad_heads, task * half, half, axis=1)
    return (
        head_out,
        grad_inputs.reshape(inputs.shape),
        grad_reduce.astype(full),
        grad_spatial.reshape(w_spatial.shape).astype(full),
        grad_expand.astype(full),
        grad_heads.astype(full)[None],
        vec_one[9],
        vec_one[8],
        vec_two[9],
        vec_two[8],
        vec_three[9],
        vec_three[8],
    )


def solution(mesh):
    in_specs = (
        P("task", "batch", None, None),
        P("task", "batch", None),
        P("task", "batch", None, None),
        P(),
        P(),
        P(),
        P("task", None, None),
        P(),
        P(),
        P(),
        P(),
        P(),
        P(),
        P("task", None, "batch", None, None),
    )
    out_specs = (
        P("task", None, "batch", None, None),
        P("task", "batch", None, None),
        P(),
        P(),
        P(),
        P("task", None, None),
        P(),
        P(),
        P(),
        P(),
        P(),
        P(),
    )
    return jax.shard_map(body, mesh=mesh, in_specs=in_specs, out_specs=out_specs, check_vma=False)
```

profile of v0, /device:TPU:0, one launch (start us, length us, event | category | flops | bytes accessed | tf_op | source)
XLA Modules:
  0.0 326.8 jit_solution(6072960869360927218)
XLA Ops:
  0.6 0.0 copy-start.10
  0.7 3.0 dynamic-slice_bitcast_fusion
  3.7 0.0 copy-done.10
  3.7 0.1 fusion.1
  3.8 0.1 slice.33
  3.8 0.1 broadcast_in_dim.54
  3.9 0.3 broadcast_in_dim.55
  4.3 0.0 copy-start.6
  4.3 0.0 copy-start.7
  4.3 0.0 copy-start.8
  4.3 0.0 copy-start.9
  4.3 0.1 slice.36
  4.4 0.1 broadcast_in_dim.59
  4.5 0.1 broadcast_in_dim.60
  4.6 0.3 broadcast_in_dim.61
  5.0 0.1 broadcast_in_dim.51
  5.1 0.3 broadcast_in_dim.52
  5.4 0.1 broadcast_in_dim.56
  5.5 0.1 broadcast_in_dim.57
  5.6 0.3 broadcast_in_dim.58
  6.0 2.0 add_convert_fusion.refs_2_.refs_4_
  8.0 0.1 pad.26.clone
  8.1 0.0 copy-done.6
  8.1 0.0 copy-done.7
  8.1 0.0 copy-done.8
  8.1 0.0 copy-done.9
  8.1 0.7 maximum_maximum_fusion.2
  8.8 20.8 %squeeze.38 = (f32[2048,512]{1,0:T(8,128)}, f32[16,512]{1,0:T(8,128)}) custom-call(bf16[2048,2048]{1,0:T(8,128)(2,1)} %bitcast.34, bf16[2048,512]{1,0:T(8,128)(2,1)} %refs_8_.1, f32[8,512]{1,0:T(8,128)} %get-tuple-element.73.refs_2_), custom_call_target="tpu_custom_call" | custom-call | tf_op jit(solution)/shard_map/squeeze/pallas_call | solution.py:686
  29.6 0.0 copy-start.4
  29.6 0.0 copy-start.5
  29.6 33.1 %mesh_forward.1 = (f32[2048,512]{1,0:T(8,128)}, bf16[1536,2048]{1,0:T(8,128)(2,1)}, f32[16,512]{1,0:T(8,128)}, bf16[2048,256]{1,0:T(8,128)(2,1)}) custom-call(f32[2048,512]{1,0:T(8,128)} %get-tuple-element.37.refs_0_.refs_2_, f32[16,512]{1,0:T(8,128)} %get-tuple-element.38.refs_1_.refs_12_, bf16[2048,512]{1,0:T(8,128)(2,1)} %add_convert_fusion.refs_2_.refs_4_, ...), custom_call_target="tpu_custom_call" | custom-call | tf_op jit(solution)/shard_map/mesh_forward/pallas_call | solution.py:686
  62.8 0.7 maximum_maximum_fusion.refs_3_
  63.5 36.2 %widen.1 = (f32[2048,2048]{1,0:T(8,128)}, bf16[512,2048]{1,0:T(8,128)(2,1)}, f32[16,2048]{1,0:T(8,128)}, bf16[2048,256]{1,0:T(8,128)(2,1)}) custom-call(f32[2048,512]{1,0:T(8,128)} %get-tuple-element.39.refs_0_.refs_3_.refs_1_, f32[16,512]{1,0:T(8,128)} %get-tuple-element.40.refs_1_.refs_4_.refs_7_, bf16[512,2048]{1,0:T(8,128)(2,1)} %refs_6_.1, ...), custom_call_target="tpu_custom_call" | custom-call | tf_op jit(solution)/shard_map/widen/pallas_call | solution.py:686
  99.7 55.6 %crown.1 = (f32[2048,256]{1,0:T(8,128)}, bf16[2048,2048]{1,0:T(8,128)(2,1)}, bf16[2048,2048]{1,0:T(8,128)(2,1)}, bf16[2048,512]{1,0:T(8,128)(2,1)}, bf16[2048,256]{1,0:T(8,128)(2,1)}, /*index=5*/f32[16,2048]{1,0:T(8,128)}) custom-call(f32[2048,2048]{1,0:T(8,128)} %get-tuple-element.41.refs_0_, bf16[2048,2048]{1,0:T(8,128)(2,1)} %bitcast.35, ...), custom_call_target="tpu_custom_call" | custom-call | tf_op jit(solution)/shard_map/crown/pallas_call | solution.py:686
  155.3 24.1 %narrow.1 = (f32[2048,512]{1,0:T(8,128)}, bf16[512,2048]{1,0:T(8,128)(2,1)}, f32[16,512]{1,0:T(8,128)}) custom-call(bf16[2048,2048]{1,0:T(8,128)(2,1)} %get-tuple-element.47.refs_0_.refs_7_, bf16[2048,2048]{1,0:T(8,128)(2,1)} %get-tuple-element.48.refs_1_, f32[16,2048]{1,0:T(8,128)} %get-tuple-element.49.refs_2_, ...), custom_call_target="tpu_custom_call" | custom-call | tf_op jit(solution)/shard_map/narrow/pallas_call | solution.py:686
  179.4 116.4 %back.1 = (bf16[2048,2048]{1,0:T(8,128)(2,1)}, bf16[2048,512]{1,0:T(8,128)(2,1)}, bf16[512,2048]{1,0:T(8,128)(2,1)}, bf16[4608,512]{1,0:T(8,128)(2,1)}, bf16[2048,512]{1,0:T(8,128)(2,1)}, /*index=5*/f32[16,512]{1,0:T(8,128)}) custom-call(f32[2048,512]{1,0:T(8,128)} %get-tuple-element.51.refs_0_, f32[2048,512]{1,0:T(8,128)} %get-tuple-element.39.refs_0_.refs_3_.refs_1_, ...), custom_call_target="tpu_custom_call" | custom-call | tf_op jit(solution)/shard_map/back/pallas_call | solution.py:1007
  295.8 0.0 copy-start.1
  295.8 7.5 %convert.2 = f32[9,512,512]{2,1,0:T(8,128)} convert(bf16[9,512,512]{2,1,0:T(8,128)(2,1)} %bitcast.42) | non-fusion elementwise | flops 2359296 | bytes 14155776 | tf_op jit(solution)/shard_map/convert_element_type | solution.py:1096
  303.3 2.6 convert_element_type.25
  305.9 0.0 copy-done
  305.9 2.5 convert_element_type.28
  308.4 2.9 bitcast_convert_fusion
  311.3 1.4 fusion.6
  312.7 1.4 fusion.5
  314.1 0.3 convert_select_fusion.1
  314.4 2.4 pad_maximum_fusion
  316.8 1.5 fusion.4
  318.3 8.4 %copy.27 = bf16[1,8,256,2048]{3,2,1,0:T(8,128)(2,1)} copy(bf16[1,8,256,2048]{3,2,1,0:T(8,128)(2,1)} %bitcast.38) | data formatting | bytes 16777216
  (17 shorter events, 0.1 us)
Async XLA Ops:
  0.6 3.0 copy-start.10
  4.3 3.8 %copy-start.6 = (f32[512]{0:T(512)S(1)}, f32[512]{0:T(512)}, u32[]{:S(2)}) copy-start(f32[512]{0:T(512)} %param.24) | copy-start | bytes 6148
  4.3 3.8 %copy-start.7 = (f32[512]{0:T(512)S(1)}, f32[512]{0:T(512)}, u32[]{:S(2)}) copy-start(f32[512]{0:T(512)} %param.23) | copy-start | bytes 6148
  4.3 3.8 %copy-start.8 = (f32[512]{0:T(512)S(1)}, f32[512]{0:T(512)}, u32[]{:S(2)}) copy-start(f32[512]{0:T(512)} %param.22) | copy-start | bytes 6148
  4.3 3.8 %copy-start.9 = (f32[512]{0:T(512)S(1)}, f32[512]{0:T(512)}, u32[]{:S(2)}) copy-start(f32[512]{0:T(512)} %param.21) | copy-start | bytes 6148
  29.6 33.2 %copy-start.4 = (f32[2048]{0:T(1024)S(1)}, f32[2048]{0:T(1024)}, u32[]{:S(2)}) copy-start(f32[2048]{0:T(1024)} %param.26) | copy-start | bytes 24580
  29.6 33.2 %copy-start.5 = (f32[2048]{0:T(1024)S(1)}, f32[2048]{0:T(1024)}, u32[]{:S(2)}) copy-start(f32[2048]{0:T(1024)} %param.25) | copy-start | bytes 24580
  295.8 7.5 %copy-start.1 = (bf16[2048,512]{1,0:T(8,128)(2,1)S(1)}, bf16[2048,512]{1,0:T(8,128)(2,1)}, u32[]{:S(2)}) copy-start(bf16[2048,512]{1,0:T(8,128)(2,1)} %get-tuple-element.57) | copy-start | bytes 6291460
  303.3 2.6 copy-start
  308.4 5.6 %copy-start.2 = (f32[2048,256]{1,0:T(8,128)S(1)}, f32[2048,256]{1,0:T(8,128)}, u32[]{:S(2)}) copy-start(f32[2048,256]{1,0:T(8,128)} %get-tuple-element.45) | copy-start | bytes 6291460
  308.4 5.6 %copy-start.3 = (bf16[2048,256]{1,0:T(8,128)(2,1)S(1)}, bf16[2048,256]{1,0:T(8,128)(2,1)}, u32[]{:S(2)}) copy-start(bf16[2048,256]{1,0:T(8,128)(2,1)} %get-tuple-element.46) | copy-start | bytes 3145732
where the time goes:
time: 328 us; the launch traced here: 327 us
  Pallas kernels  286 us (87%)
  other arithmetic  21.8 us (7%)
  local copies, waits for them, and re-layouts  18 us (5%)
    pallas_call x5, Pallas kernels, tiled(): pl.pallas_call(run, grid=(rows // tile,), out_shape=out_shape, in_specs=i...  170 us
    pallas_call x1, Pallas kernels, back(): pl.pallas_call(functools.partial(back_kernel, rows, tasks, batch, tile),...  116 us
    unnamed x23, local copies, waits for them, and re-layouts  8.5 us
    convert_element_type x1, other arithmetic, body(): grad_spatial.reshape(w_spatial.shape).astype(full)  7.52 us

commit v1 on v0

--- a/solution.py
+++ b/solution.py
@@ -47,12 +47,7 @@
     "red1": ((1, 6), (5, 0),),
     "red2": ((3, 4), (5, 1),),
     "red3": ((6, 0),),
-    "inp0": ((0, 7), (4, 4), (6, 1),),
-    "inp2": ((0, 8), (2, 5),),
-    "inp3": ((1, 7),),
-    "inp5": ((1, 8), (3, 5), (5, 2),),
-    "inp7": ((6, 2), (4, 5),),
-    "tail": ((2, 6), (3, 6), (5, 3), (6, 3), (4, 6), (5, 4), (2, 7), (6, 4), (2, 8), (3, 7), (5, 5), (3, 8), (6, 5), (4, 7), (5, 6), (4, 8), (6, 6), (5, 7), (5, 8), (6, 7), (6, 8),),
+    "tail": ((4, 4), (0, 7), (6, 1), (0, 8), (2, 5), (1, 7), (3, 5), (5, 2), (1, 8), (6, 2), (4, 5), (2, 6), (3, 6), (5, 3), (6, 3), (4, 6), (5, 4), (2, 7), (6, 4), (2, 8), (3, 7), (5, 5), (3, 8), (6, 5), (4, 7), (5, 6), (4, 8), (6, 6), (5, 7), (5, 8), (6, 7), (6, 8),),
 }
 
 
@@ -410,12 +405,14 @@
 
 
 def crown_kernel(
-    piece, h_ref, x_ref, thr_ref, cot_ref, cot_peer_ref, top_ref, top_peer_ref, vec_ref,
+    piece, h_ref, x_ref, thr_ref, cot_hbm, cot_one, cot_two, top_ref, top_one, top_two, vec_ref,
     out_ref, flow_ref, normed_ref, grad_ref, came_ref, stat_ref, z_ref, acc_ref, sent_ref, sems,
+    cots_ref, cots_peer_ref, top_peer_ref, local_sems, late_sems,
 ):
     step = pl.program_id(0)
     rows, width = x_ref.shape
-    half = cot_ref.shape[1]
+    all_rows, half = cots_ref.shape
+    split = all_rows // 4
     task = lax.axis_index("task")
     last = pl.num_programs(0) - 1
 
@@ -423,9 +420,39 @@
         span = pl.ds(pl.multiple_of(index * rows, rows), rows)
         return across(sent_ref.at[span], came_ref.at[span], sems.at[index])
 
+    core = lax.rem(lax.axis_index("batch"), 2)
+    high = top_one.shape[0]
+    late = across(cot_hbm.at[1 - task, pl.ds(2 * split, 2 * split)], cots_peer_ref.at[pl.ds(2 * split, 2 * split)], late_sems)
+
+    @pl.when(step == 0)
+    def _():
+        pairs = [
+            (cot_hbm.at[task], cots_ref),
+            (cot_one, cots_peer_ref.at[pl.ds(0, split)]),
+            (cot_two, cots_peer_ref.at[pl.ds(split, split)]),
+            (top_one, top_peer_ref.at[pl.ds(pl.multiple_of(core * high, high), high)]),
+            (top_two, top_peer_ref.at[pl.ds(pl.multiple_of((1 - core) * high, high), high)]),
+        ]
+        copies = [pltpu.make_async_copy(a, b, local_sems.at[i]) for i, (a, b) in enumerate(pairs)]
+        for copy in copies:
+            copy.start()
+        for copy in copies:
+            copy.wait()
+
+    @pl.when(step == 1)
+    def _():
+        late.start()
+
+    @pl.when(step == (last + 1) // 2)
+    def _():
+        late.wait()
+
     @pl.when(step > 0)
     def _():
         send(step - 1).start()
+
+    span = pl.ds(pl.multiple_of(step * rows, rows), rows)
+    cot_ref, cot_peer_ref = cots_ref.at[span], cots_peer_ref.at[span]
 
     @pl.when(step == 0)
     def _():
@@ -590,18 +617,21 @@
     return part(0), part(1)
 
 
-def across(source, target, sems):
+def across(source, target, sems, hop="task"):
+    task = lax.axis_index("task")
+    place = lax.axis_index("batch")
+    device = (1 - task, place) if hop == "task" else (task, place + 1 - 2 * lax.rem(place, 2))
     return pltpu.make_async_remote_copy(
         src_ref=source,
         dst_ref=target,
         send_sem=sems.at[0],
         recv_sem=sems.at[1],
-        device_id=(1 - lax.axis_index("task"), lax.axis_index("batch")),
+        device_id=device,
         device_id_type=MESH,
     )
 
 
-def tiled(kernel, tile, moving, flags, outs, fixed, scratch, name, stats=None, send=None, far=(), fill=None, turns=()):
+def tiled(kernel, tile, moving, flags, outs, fixed, scratch, name, stats=None, sends=(), far=(), fill=None, turns=()):
     tasks = lax.axis_size("task")
     batch = lax.axis_size("batch")
     rows = moving[0].shape[0]
@@ -618,7 +648,7 @@
 
     hbm = pl.BlockSpec(memory_space=pl.ANY)
     operands = list(moving)
-    in_specs = [block(a) if m else whole(a) for a, m in zip(moving, flags)]
+    in_specs = [(whole, block, lambda a: hbm)[m](a) for a, m in zip(moving, flags)]
     out_shape = outs + fixed + list(far)
     out_specs = [turned(a) if i in turns else block(a) for i, a in enumerate(outs)] + [whole(a) for a in fixed] + [hbm for a in far]
     scratch = list(scratch)
@@ -635,10 +665,10 @@
         out_specs = out_specs + [whole(out_shape[-1])]
         scratch = scratch + [pltpu.VMEM((24 if forward else 16, width), jnp.float32)]
         scratch = scratch + Exchange.scratch(tasks, batch, width)
-        if send is not None:
-            operands.append(send)
+        for array, _, shape, _ in sends:
+            operands.append(array)
             in_specs.append(hbm)
-            out_shape = out_shape + [jax.ShapeDtypeStruct(send.shape, send.dtype)]
+            out_shape = out_shape + [jax.ShapeDtypeStruct(shape, array.dtype)]
             out_specs = out_specs + [hbm]
             scratch = scratch + [pltpu.SemaphoreType.DMA((2,))]
 
@@ -647,10 +677,10 @@
             take = lambda n: [refs.pop(0) for _ in range(n)]
             used = take(ins)
             vec_ref = take(1)[0]
-            source = take(1)[0] if send is not None else None
+            sources = take(len(sends))
             given = take(made)
             out_ref = take(1)[0]
-            target = take(1)[0] if send is not None else None
+            targets = take(len(sends))
             own = take(held)
             stat_ref = take(1)[0]
             exchange = Exchange(tasks, batch, *take(6))
@@ -661,14 +691,18 @@
             def _():
                 exchange.greet()
 
-            early = send is not None or len(far) > 0
+            early = len(sends) > 0 or len(far) > 0
+
+            def crossing(index):
+                _, view, _, hop = sends[index]
+                return across(view(sources[index]), targets[index], refs[index], hop)
             if early:
 
                 @pl.when(step == 1)
                 def _():
                     exchange.met()
-                    if send is not None:
-                        across(source, target, refs[0]).start()
+                    for index in range(len(sends)):
+                        crossing(index).start()
 
             after = kernel(*used, *given, stat_ref, *own)
 
@@ -678,8 +712,8 @@
                     exchange.met()
                 fillers = (None, None) if fill is None else fill(*used, *given, stat_ref, *own)
                 settle_stats(exchange, stat_ref, vec_ref, out_ref, rows, rows * tasks * batch, forward, fillers)
-                if send is not None:
-                    across(source, target, refs[0]).wait()
+                for index in range(len(sends)):
+                    crossing(index).wait()
                 if after is not None:
                     after()
 
@@ -708,21 +742,21 @@
     return tiled(squeeze_kernel, tile, [flat_in, w_reduce], [1, 0], [shape32(rows, mid)], [], [], "squeeze", stats)
 
 
-def mesh_forward(h_one, vec, masks, taps, stats, send, tile):
+def mesh_forward(h_one, vec, masks, taps, stats, sends, tile):
     rows, mid = h_one.shape
     return tiled(
         mesh_kernel, tile, [h_one, vec, masks, taps], [1, 0, 1, 0],
         [shape32(rows, mid), shape16(3 * mid, rows)], [],
-        [pltpu.VMEM((tile + 2 * SIDE, 3 * mid), jnp.bfloat16)], "mesh_forward", stats, send, turns=(1,),
-    )
-
-
-def widen(h_two, vec, w_expand, stats, send, tile):
+        [pltpu.VMEM((tile + 2 * SIDE, 3 * mid), jnp.bfloat16)], "mesh_forward", stats, sends, turns=(1,),
+    )
+
+
+def widen(h_two, vec, w_expand, stats, sends, tile):
     rows, mid = h_two.shape
     width = w_expand.shape[1]
     return tiled(
         widen_kernel, tile, [h_two, vec, w_expand], [1, 0, 0],
-        [shape32(rows, width), shape16(mid, rows)], [], [], "widen", stats, send, turns=(1,),
+        [shape32(rows, width), shape16(mid, rows)], [], [], "widen", stats, sends, turns=(1,),
     )
 
 
@@ -736,20 +770,25 @@
     )
 
 
-def crown(h_three, flat_in, limits, cot, cot_peer, top, top_peer, vec, stats, tile, piece):
+def crown(h_three, flat_in, limits, cots, cot_parts, top, top_parts, vec, stats, tile, piece):
     rows, width = flat_in.shape
-    half = cot.shape[1]
+    half = cots.shape[2]
     return tiled(
         functools.partial(crown_kernel, piece), tile,
-        [h_three, flat_in, limits, cot, cot_peer, top, top_peer, vec], [1, 1, 1, 1, 1, 0, 0, 0],
+        [h_three, flat_in, limits, cots, *cot_parts, top, *top_parts, vec], [1, 1, 1, 2, 2, 2, 0, 2, 2, 0],
         [shape32(rows, half), shape16(rows, width), shape16(rows, width)], [shape16(width, 2 * half)],
         [
             pltpu.VMEM((tile, width), jnp.bfloat16),
             pltpu.VMEM((2 * half, width), jnp.float32),
             pltpu.VMEM((rows, half), jnp.bfloat16),
             pltpu.SemaphoreType.DMA((rows // tile, 2)),
+            pltpu.VMEM((rows, half), jnp.bfloat16),
+            pltpu.VMEM((rows, half), jnp.bfloat16),
+            pltpu.VMEM((width, half), jnp.bfloat16),
+            pltpu.SemaphoreType.DMA((5,)),
+            pltpu.SemaphoreType.DMA((2,)),
         ],
-        "crown", stats, None, [shape16(rows, half)],
+        "crown", stats, (), [shape16(rows, half)],
     )
 
 
@@ -780,12 +819,11 @@
     def take(count):
         return [refs.pop(0) for _ in range(count)]
 
-    (flow_hbm, two_hbm, one_hbm, side_hbm, mask_hbm, w_hbm, x_hbm, up_hbm, top_hbm, heads_hbm, expand_hbm) = take(11)
+    (flow_hbm, two_hbm, one_hbm, side_hbm, mask_hbm, w_hbm, x_hbm, heads_hbm, expand_hbm) = take(9)
     vectwo_ref, vecone_ref = take(2)
     (out_hbm, heads_out, expand_out, spatial_out, reduce_out, vec_ref) = take(6)
-    (two_buf, mask_buf, x_buf, up_buf, out_buf) = take(5)
-    (side_ref, lane_ref, flow_ref, w_ref, top_ref) = take(5)
-    small = up_buf.shape[1]
+    (two_buf, mask_buf, x_buf) = take(3)
+    (side_ref, lane_ref, flow_ref, w_ref) = take(4)
     heads_work, expand_work, spatial_work, reduce_work, stat_ref = take(5)
     pair_sems, whole_sems, flow_sems = take(3)
     exchange = Exchange(tasks, batch, *take(6))
@@ -807,20 +845,20 @@
     twos = Stream(blocks(two_hbm, tile), two_buf, pair_sems.at[1])
     masks = Stream(blocks(mask_hbm, tile), mask_buf, pair_sems.at[2])
     ones = Stream(blocks(one_hbm, tile), two_buf, pair_sems.at[3])
-    ups = Stream(blocks(up_hbm, small), up_buf, pair_sems.at[4])
     dh_ref, normed_ref, dht_ref = lane_ref.at[:, :mid], lane_ref.at[:, mid : 2 * mid], side_ref.at[:mid]
     across_cols = x_buf.shape[2]
     columns = Stream(
         lambda index: x_hbm.at[:, pl.ds(pl.multiple_of(index * across_cols, across_cols), across_cols)],
-        x_buf, pair_sems.at[5],
+        x_buf, pair_sems.at[0],
     )
     loads = [
         pltpu.make_async_copy(source, target, whole_sems.at[index])
         for index, (source, target) in enumerate(
-            [(heads_hbm, heads_work), (side_hbm, side_ref), (expand_hbm, expand_work), (w_hbm, w_ref), (top_hbm, top_ref)]
+            [(heads_hbm, heads_work), (side_hbm, side_ref), (expand_hbm, expand_work), (w_hbm, w_ref)]
         )
     ]
-    heads_load, side_load, expand_load, w_load, top_load = loads
+    heads_load, side_load, expand_load, w_load = loads
+    keep = pltpu.make_async_copy(dh_ref, out_hbm, whole_sems.at[4])
     heads_load.start()
     for stream in (twos, masks):
         stream.start(0)
@@ -918,7 +956,6 @@
 
     lax.fori_loop(0, spans, taps, 0)
     columns.start(0)
-    ups.start(0)
     settle_stats(exchange, stat_ref, vecone_ref, vec_ref, rows, rows * tasks * batch, False)
     tick("xch")
 
@@ -930,6 +967,7 @@
         return carry
 
     lax.fori_loop(0, spans, inner, 0)
+    keep.start()
     tick("inner")
     count = width // across_cols
 
@@ -941,36 +979,11 @@
         return carry
 
     lax.fori_loop(0, count, reduce, 0)
-    top_load.wait()
-
-    def store(index):
-        slot = lax.rem(index, 2)
-        return pltpu.make_async_copy(out_buf.at[slot], blocks(out_hbm, small)(index), pair_sems.at[6, slot])
-
-    def inputs(index, carry):
-        span = pl.ds(pl.multiple_of(index * small, small), small)
-        up = ups.take(index, rows // small)
-
-        @pl.when(index >= 2)
-        def _():
-            store(index - 2).wait()
-
-        slot = lax.rem(index, 2)
-        for start in range(0, width, across_cols):
-            cols = pl.ds(start, across_cols)
-            part = lax.dot_general(dh_ref[span], top_ref[cols], COLS_COLS, preferred_element_type=jnp.float32)
-            out_buf[slot, :, cols] = (up[:, cols].astype(jnp.float32) + part).astype(jnp.bfloat16)
-        store(index).start()
-        ticks("inp", index, 8)
-        return carry
-
-    lax.fori_loop(0, rows // small, inputs, 0)
-    for index in range(rows // small - 2, rows // small):
-        store(index).wait()
+    keep.wait()
     tick("tail")
 
 
-def back(flow, h_two, vec_two, h_one, vec_one, sides, masks, w_spatial, flat_in, up, w_reduce, heads, expand, ident, tile):
+def back(flow, h_two, vec_two, h_one, vec_one, sides, masks, w_spatial, flat_in, heads, expand, ident, tile):
     tasks = lax.axis_size("task")
     batch = lax.axis_size("batch")
     far = batch // LOW
@@ -986,19 +999,16 @@
         pltpu.VMEM((2, tile, mid), full),
         pltpu.VMEM((2, tile, 512), low),
         pltpu.VMEM((2, rows, cols), low),
-        pltpu.VMEM((2, 256, width), low),
-        pltpu.VMEM((2, 256, width), low),
         pltpu.VMEM((3 * mid, rows), low),
         pltpu.VMEM((rows, 3 * mid), low),
         pltpu.VMEM((rows, mid), full),
         pltpu.VMEM(w_spatial.shape, low),
-        pltpu.VMEM(w_reduce.shape, low),
         pltpu.VMEM(heads.shape, low),
         pltpu.VMEM(expand.shape, low),
         pltpu.VMEM((9 * mid, mid), low),
         pltpu.VMEM((width, mid), low),
         pltpu.VMEM((16, mid), full),
-        pltpu.SemaphoreType.DMA((7, 2)),
+        pltpu.SemaphoreType.DMA((4, 2)),
         pltpu.SemaphoreType.DMA((5,)),
         pltpu.SemaphoreType.DMA((rows // tile,)),
     ] + Exchange.scratch(tasks, batch, mid)
@@ -1007,17 +1017,66 @@
     return pl.pallas_call(
         functools.partial(back_kernel, rows, tasks, batch, tile),
         out_shape=[
-            shape16(rows, width), shape16(*heads.shape), shape16(*expand.shape), shape16(9 * mid, mid),
+            shape16(rows, mid), shape16(*heads.shape), shape16(*expand.shape), shape16(9 * mid, mid),
             shape16(width, mid), shape32(16, mid),
         ],
-        in_specs=[hbm] * 11 + [vmem] * 2,
+        in_specs=[hbm] * 9 + [vmem] * 2,
         out_specs=[hbm] * 5 + [vmem],
         scratch_shapes=scratch,
         compiler_params=pltpu.CompilerParams(
             vmem_limit_bytes=VMEM_BYTES, collective_id=ident, has_side_effects=True
         ),
         name="back",
-    )(flow, h_two, h_one, sides, masks, w_spatial, flat_in, up, w_reduce, heads, expand, vec_two, vec_one)
+    )(flow, h_two, h_one, sides, masks, w_spatial, flat_in, heads, expand, vec_two, vec_one)
+
+
+def finish_kernel(
+    dh_ref, up_ref, heads_ref, expand_ref, spatial_ref, reduce_ref, mine_ref, came_ref, w_ref, one_ref, two_ref, three_ref,
+    out_ref, heads_out, expand_out, spatial_out, reduce_out, both_ref, *sums,
+):
+    full = jnp.float32
+    task = lax.axis_index("task")
+    half = heads_out.shape[1]
+    back = lax.dot_general(dh_ref[...], w_ref[...], COLS_COLS, preferred_element_type=full)
+    out_ref[...] = (up_ref[...].astype(full) + back).astype(jnp.bfloat16)
+    heads_out[...] = jnp.where(task == 0, heads_ref[:, :half], heads_ref[:, half:]).astype(full)
+    expand_out[...] = expand_ref[...].astype(full)
+    spatial_out[...] = spatial_ref[...].astype(full)
+    reduce_out[...] = reduce_ref[...].astype(full)
+    both_ref[task] = mine_ref[...]
+    both_ref[1 - task] = came_ref[...].astype(full)
+
+    @pl.when(pl.program_id(0) == 0)
+    def _():
+        for index, vec_ref in enumerate((one_ref, two_ref, three_ref)):
+            sums[2 * index][...] = vec_ref[9:10]
+            sums[2 * index + 1][...] = vec_ref[8:9]
+
+
+def finish(dh, up, heads, expand, spatial, reduce, mine, came, w_reduce, vecs, steps):
+    def block(array, lead=0):
+        zeros = (0,) * (len(array.shape) - 1 - lead)
+        height = array.shape[lead] // steps
+        return pl.BlockSpec(array.shape[:lead] + (height,) + array.shape[lead + 1 :], lambda i: (0,) * lead + (i,) + zeros)
+
+    def whole(array):
+        return pl.BlockSpec(array.shape, lambda i: (0, 0))
+
+    rows, half = mine.shape
+    moving = [dh, up, heads, expand, spatial, reduce, mine, came]
+    fixed = [w_reduce, *vecs]
+    outs = [shape16(*up.shape), shape32(heads.shape[0], half), shape32(*expand.shape), shape32(*spatial.shape), shape32(*reduce.shape)]
+    both = shape32(2, rows, half)
+    sums = [shape32(1, vec.shape[1]) for vec in vecs for _ in range(2)]
+    return pl.pallas_call(
+        finish_kernel,
+        grid=(steps,),
+        out_shape=outs + [both] + sums,
+        in_specs=[block(a) for a in moving] + [whole(a) for a in fixed],
+        out_specs=[block(a) for a in outs] + [block(both, 1)] + [whole(a) for a in sums],
+        compiler_params=pltpu.CompilerParams(vmem_limit_bytes=VMEM_BYTES),
+        name="finish",
+    )(*moving, *fixed)
 
 
 def body(
@@ -1042,10 +1101,7 @@
     mid = w_reduce.shape[1]
     rows = canvases * pixels
     half = w_heads.shape[2]
-    task = lax.axis_index("task")
-    cot = cotangent.reshape(2, rows, half)
-    cot_mine = lax.dynamic_index_in_dim(cot, task, 0, keepdims=False)
-    cot_sent = lax.dynamic_index_in_dim(cot, 1 - task, 0, keepdims=False)
+    cots = cotangent.reshape(2, rows, half)
     top_mine = w_heads[0]
 
     def params(gain, bias):
@@ -1066,42 +1122,48 @@
     ).astype(low).reshape(rows, 512)
 
     flat_in = inputs.reshape(rows, width)
+    core = lambda: lax.rem(lax.axis_index("batch"), 2)
+    other = lambda: 1 - lax.axis_index("task")
+    quarter = rows // 4
+    top_rows = width // 2
     h_one, vec_one = squeeze(flat_in, w_reduce, (params(gain_one, bias_one), True, 0), min(rows, 512))
-    h_two, sides, vec_two, cot_peer = mesh_forward(
-        h_one, vec_one, masks, w_spatial.reshape(9 * mid, mid), (params(gain_two, bias_two), True, 1), cot_sent, pixels
-    )
-    h_three, q_two, vec_three, top_peer = widen(
-        h_two, vec_two, w_expand, (params(gain_three, bias_three), True, 2), top_mine, pixels
+    sends = [
+        (top_mine, lambda ref: ref.at[pl.ds(pl.multiple_of(core() * top_rows, top_rows), top_rows)], (top_rows, half), "task"),
+        (cots, lambda ref: ref.at[other(), pl.ds(0, quarter)], (quarter, half), "task"),
+    ]
+    h_two, sides, vec_two, top_one, cot_one = mesh_forward(
+        h_one, vec_one, masks, w_spatial.reshape(9 * mid, mid), (params(gain_two, bias_two), True, 1), sends, pixels
+    )
+    sends = [
+        (top_one, lambda ref: ref, (top_rows, half), "core"),
+        (cots, lambda ref: ref.at[other(), pl.ds(quarter, quarter)], (quarter, half), "task"),
+    ]
+    h_three, q_two, vec_three, top_two, cot_two = widen(
+        h_two, vec_two, w_expand, (params(gain_three, bias_three), True, 2), sends, pixels
     )
     out_mine, flow, normed, grad_heads, out_peer, vec_three = crown(
-        h_three, flat_in, threshold.reshape(rows, width), cot_mine, cot_peer, top_mine, top_peer, vec_three,
+        h_three, flat_in, threshold.reshape(rows, width), cots, (cot_one, cot_two), top_mine, (top_one, top_two), vec_three,
         (vec_three, False, 3), pixels, 256,
     )
-    out_peer = out_peer.astype(full)
-    first = jnp.where(task == 0, out_mine, out_peer)
-    second = jnp.where(task == 0, out_peer, out_mine)
-    head_out = jnp.stack([first, second]).reshape(1, 2, canvases, pixels, half)
     flow_two, grad_expand, vec_two = narrow(
         flow, normed, vec_three, h_two, vec_two, q_two, w_expand, (vec_two, False, 4), min(rows, 512)
     )
-    grad_inputs, grad_heads, grad_expand, grad_spatial, grad_reduce, vec_one = back(
-        flow_two, h_two, vec_two, h_one, vec_one, sides, masks, w_spatial, flat_in, flow, w_reduce,
-        grad_heads, grad_expand, 5, min(rows, 512),
-    )
-    grad_heads = lax.dynamic_slice_in_dim(grad_heads, task * half, half, axis=1)
+    dh_one, grad_heads, grad_expand, grad_spatial, grad_reduce, vec_one = back(
+        flow_two, h_two, vec_two, h_one, vec_one, sides, masks, w_spatial, flat_in, grad_heads, grad_expand, 5,
+        min(rows, 512),
+    )
+    grad_inputs, grad_heads, grad_expand, grad_spatial, grad_reduce, head_out, *sums = finish(
+        dh_one, flow, grad_heads, grad_expand, grad_spatial, grad_reduce, out_mine, out_peer, w_reduce,
+        (vec_one, vec_two, vec_three), 8,
+    )
     return (
-        head_out,
+        head_out.reshape(1, 2, canvases, pixels, half),
         grad_inputs.reshape(inputs.shape),
-        grad_reduce.astype(full),
-        grad_spatial.reshape(w_spatial.shape).astype(full),
-        grad_expand.astype(full),
-        grad_heads.astype(full)[None],
-        vec_one[9],
-        vec_one[8],
-        vec_two[9],
-        vec_two[8],
-        vec_three[9],
-        vec_three[8],
+        grad_reduce,
+        grad_spatial.reshape(w_spatial.shape),
+        grad_expand,
+        grad_heads[None],
+        *[row.reshape(-1) for row in sums],
     )
 
 

time: 328 us -> 303 us (0.924)
  other arithmetic: 21.8 us -> 4.94 us
  local copies, waits for them, and re-layouts: 18 us -> 2.92 us
  Pallas kernels: 286 us -> 294 us
    pallas_call x0 -> x1, Pallas kernels: none -> 22.6 us  [finish(): pl.pallas_call(finish_kernel, grid=(steps,), out_shape=outs + [both] + su...]
    pallas_call x5, Pallas kernels: 170 us -> 154 us  [tiled(): pl.pallas_call(run, grid=(rows // tile,), out_shape=out_shape, in_specs=i...]
    convert_element_type x3 -> x0, other arithmetic: 12.7 us -> none  [the longest x1 7.52 us: body(): grad_spatial.reshape(w_spatial.shape).astype(full)]
    unnamed x23 -> x0, local copies, waits for them, and re-layouts: 8.5 us -> none
    slice x3 -> x0, local copies, waits for them, and re-layouts: 4.28 us -> none  [the longest x1 1.53 us: body(): vec_three[8]]
where the time goes in v1:
time: 303 us; the launch traced here: 302 us
  Pallas kernels  294 us (97%)
  other arithmetic  4.94 us (2%)
    pallas_call x5, Pallas kernels, tiled(): pl.pallas_call(run, grid=(rows // tile,), out_shape=out_shape, in_specs=i...  154 us
    pallas_call x1, Pallas kernels, back(): pl.pallas_call(functools.partial(back_kernel, rows, tasks, batch, tile),...  117 us
    pallas_call x1, Pallas kernels, finish(): pl.pallas_call(finish_kernel, grid=(steps,), out_shape=outs + [both] + su...  22.6 us

profile of v1, /device:TPU:0, one launch (start us, length us, event | category | flops | bytes accessed | tf_op | source)
XLA Modules:
  0.0 302.5 jit_solution(8921792617616578304)
XLA Ops:
  0.7 0.1 pad.24.clone
  0.7 0.8 slice_bitcast_fusion.1
  1.5 0.1 fusion.1
  1.6 0.1 slice.15
  1.7 0.1 slice.18
  1.7 0.1 broadcast_in_dim.56
  1.8 0.1 broadcast_in_dim.57
  1.9 0.1 broadcast_in_dim.53
  2.0 0.1 broadcast_in_dim.54
  2.1 0.1 broadcast_in_dim.51
  2.3 0.1 broadcast_in_dim.48
  2.4 1.4 maximum_maximum_fusion.2
  3.8 1.4 maximum_maximum_fusion.refs_3_
  5.2 0.3 broadcast_in_dim.49
  5.5 0.3 broadcast_in_dim.52
  5.9 0.3 broadcast_in_dim.55
  6.2 0.3 broadcast_in_dim.58
  6.6 2.0 add_convert_fusion.refs_2_.refs_4_
  8.6 20.8 %squeeze.5 = (f32[2048,512]{1,0:T(8,128)}, f32[16,512]{1,0:T(8,128)}) custom-call(bf16[2048,2048]{1,0:T(8,128)(2,1)} %bitcast.26, bf16[2048,512]{1,0:T(8,128)(2,1)} %w_ref.1, f32[8,512]{1,0:T(8,128)} %get-tuple-element.91.refs_2_), custom_call_target="tpu_custom_call" | custom-call | tf_op jit(solution)/shard_map/squeeze/pallas_call | solution.py:720
  29.4 28.5 %mesh_forward.1 = (f32[2048,512]{1,0:T(8,128)}, bf16[1536,2048]{1,0:T(8,128)(2,1)}, f32[16,512]{1,0:T(8,128)}, bf16[1024,256]{1,0:T(8,128)(2,1)}, bf16[512,256]{1,0:T(8,128)(2,1)}) custom-call(f32[2048,512]{1,0:T(8,128)} %get-tuple-element.51.refs_0_.refs_2_, f32[16,512]{1,0:T(8,128)} %get-tuple-element.52.refs_1_.refs_10_, ...), custom_call_target="tpu_custom_call" | custom-call | tf_op jit(solution)/shard_map/mesh_forward/pallas_call | solution.py:720
  57.9 23.9 %widen.1 = (f32[2048,2048]{1,0:T(8,128)}, bf16[512,2048]{1,0:T(8,128)(2,1)}, f32[16,2048]{1,0:T(8,128)}, bf16[1024,256]{1,0:T(8,128)(2,1)}, bf16[512,256]{1,0:T(8,128)(2,1)}) custom-call(f32[2048,512]{1,0:T(8,128)} %get-tuple-element.53.refs_0_.refs_3_.refs_1_, f32[16,512]{1,0:T(8,128)} %get-tuple-element.54.refs_1_.refs_4_.refs_7_, ...), custom_call_target="tpu_custom_call" | custom-call | tf_op jit(solution)/shard_map/widen/pallas_call | solution.py:720
  81.8 57.1 %crown.1 = (f32[2048,256]{1,0:T(8,128)}, bf16[2048,2048]{1,0:T(8,128)(2,1)}, bf16[2048,2048]{1,0:T(8,128)(2,1)}, bf16[2048,512]{1,0:T(8,128)(2,1)}, bf16[2048,256]{1,0:T(8,128)(2,1)}, /*index=5*/f32[16,2048]{1,0:T(8,128)}) custom-call(f32[2048,2048]{1,0:T(8,128)} %get-tuple-element.56.refs_0_, bf16[2048,2048]{1,0:T(8,128)(2,1)} %bitcast.27, ...), custom_call_target="tpu_custom_call" | custom-call | tf_op jit(solution)/shard_map/crown/pallas_call | solution.py:720
  138.9 24.1 %narrow.1 = (f32[2048,512]{1,0:T(8,128)}, bf16[512,2048]{1,0:T(8,128)(2,1)}, f32[16,512]{1,0:T(8,128)}) custom-call(bf16[2048,2048]{1,0:T(8,128)(2,1)} %get-tuple-element.61.refs_0_.up_ref, bf16[2048,2048]{1,0:T(8,128)(2,1)} %get-tuple-element.62.refs_1_, f32[16,2048]{1,0:T(8,128)} %get-tuple-element.63.refs_2_.three_ref, ...), custom_call_target="tpu_custom_call" | custom-call | tf_op jit(solution)/shard_map/narrow/pallas_call | solution.py:720
  163.0 116.7 %back.1 = (bf16[2048,512]{1,0:T(8,128)(2,1)}, bf16[2048,512]{1,0:T(8,128)(2,1)}, bf16[512,2048]{1,0:T(8,128)(2,1)}, bf16[4608,512]{1,0:T(8,128)(2,1)}, bf16[2048,512]{1,0:T(8,128)(2,1)}, /*index=5*/f32[16,512]{1,0:T(8,128)}) custom-call(f32[2048,512]{1,0:T(8,128)} %get-tuple-element.65.refs_0_, f32[2048,512]{1,0:T(8,128)} %get-tuple-element.53.refs_0_.refs_3_.refs_1_, ...), custom_call_target="tpu_custom_call" | custom-call | tf_op jit(solution)/shard_map/back/pallas_call | solution.py:1017
  279.7 22.6 %finish.1 = (bf16[2048,2048]{1,0:T(8,128)(2,1)}, f32[2048,256]{1,0:T(8,128)}, f32[512,2048]{1,0:T(8,128)}, f32[4608,512]{1,0:T(8,128)}, f32[2048,512]{1,0:T(8,12...) custom-call(bf16[2048,512]{1,0:T(8,128)(2,1)} %get-tuple-element.70., ...), custom_call_target="tpu_custom_call" | custom-call | tf_op jit(solution)/shard_map/finish/pallas_call | solution.py:1071
  (8 shorter events, 0.1 us)

commit v2 on v1

--- a/solution.py
+++ b/solution.py
@@ -25,64 +25,67 @@
 
 
 AGENDA = {
-    "start": ((0, 0), (1, 0),),
-    "lane1": ((0, 1),),
+    "start": ((0, 3),),
+    "lane0": ((1, 0),),
     "lane2": ((1, 1),),
+    "sp1": ((0, 4),),
     "sp2": ((2, 0),),
-    "sp3": ((0, 2),),
-    "sp4": ((2, 1),),
+    "sp4": ((1, 2), (2, 1),),
     "sp5": ((3, 0),),
-    "sp7": ((1, 2), (3, 1),),
-    "sp8": ((4, 0),),
-    "tap0": ((0, 3),),
-    "tap1": ((4, 1),),
-    "tap2": ((2, 2),),
-    "tap4": ((1, 3),),
-    "tap5": ((0, 4),),
-    "tap6": ((3, 2),),
-    "tap9": ((1, 4), (4, 2),),
-    "tap10": ((2, 3),),
-    "xch": ((0, 5), (1, 5), (3, 3), (4, 3),),
-    "inner": ((0, 6), (2, 4),),
-    "red1": ((1, 6), (5, 0),),
-    "red2": ((3, 4), (5, 1),),
-    "red3": ((6, 0),),
-    "tail": ((4, 4), (0, 7), (6, 1), (0, 8), (2, 5), (1, 7), (3, 5), (5, 2), (1, 8), (6, 2), (4, 5), (2, 6), (3, 6), (5, 3), (6, 3), (4, 6), (5, 4), (2, 7), (6, 4), (2, 8), (3, 7), (5, 5), (3, 8), (6, 5), (4, 7), (5, 6), (4, 8), (6, 6), (5, 7), (5, 8), (6, 7), (6, 8),),
+    "sp8": ((0, 5), (1, 3), (3, 1), (4, 0),),
+    "tap1": ((2, 2), (4, 1),),
+    "tap5": ((0, 7), (1, 4),),
+    "tap7": ((0, 8), (3, 2),),
+    "tap8": ((2, 3),),
+    "xch": ((1, 5), (2, 4), (3, 3), (4, 2),),
+    "inner": ((1, 6),),
+    "red1": ((2, 5), (4, 3), (5, 0),),
+    "red3": ((3, 4), (5, 1), (6, 0), (1, 7),),
+    "tail": ((2, 6), (6, 1), (4, 4), (1, 8), (5, 2), (3, 5), (2, 7), (2, 8), (6, 2), (4, 5), (5, 3), (3, 6), (6, 3), (4, 6), (5, 4), (3, 7), (6, 4), (3, 8), (5, 5), (4, 7), (6, 5), (5, 6), (4, 8), (6, 6), (5, 7), (5, 8), (6, 7), (6, 8),),
 }
 
 
 class Reduction:
-    def __init__(self, grid, work, result, core, first, second, last, done, send, recv, far_send, far_recv, local, wide):
+    def __init__(
+        self, grid, work, result, core, first_a, first_b, second, last, done, send, recv, far_send, far_recv, local,
+        kind, shape=None,
+    ):
         self.grid, self.work, self.result = grid, work, result
-        self.room, self.done = (core, first, second, last), done
+        self.core_room, self.first_rooms, self.second_room, self.last_room = core, (first_a, first_b), second, last
+        self.done = done
         self.send, self.recv, self.far_send, self.far_recv = send, recv, far_send, far_recv
         self.local = local
-        self.wide = wide
-        self.rows, self.cols = work.shape
-        sizes = self.sizes(self.rows, self.cols, wide, grid.far)
-        self.pieces = sizes[2][0] // sizes[3][0]
+        self.kind = kind
+        self.resumed = shape is not None
+        self.rows, self.cols = shape or work.shape
+        sizes = self.sizes(self.rows, self.cols, kind, grid.far)
+        self.pieces = sizes[3][0] // sizes[4][0]
         self.mine = lax.rem(grid.high, self.pieces)
 
     @staticmethod
-    def sizes(rows, cols, wide, far):
-        if wide:
-            core = (rows, cols // 2)
-            first = (rows, cols // 8)
-            second = (rows, cols // 16)
+    def sizes(rows, cols, kind, far):
+        if kind == "wide":
+            core, first, second = (rows, cols // 2), (rows, cols // 8), (rows, cols // 16)
+            firsts = first, first
+        elif kind == "tall":
+            core, first, second = (rows // 2, cols), (rows // 2, cols // 4), (rows // 4, cols // 4)
+            firsts = first, first
         else:
-            core = (rows // 2, cols)
-            first = (rows // 2, cols // 4)
-            second = (rows // 4, cols // 4)
+            core, second = (rows // 2, cols), (rows // 8, cols // 2)
+            firsts = (rows // 4, cols // 2), (rows // 8, cols)
         pieces = max(n for n in range(1, far + 1) if far % n == 0 and second[0] % (8 * n) == 0)
-        return core, first, second, (second[0] // pieces, second[1])
+        return core, *firsts, second, (second[0] // pieces, second[1])
 
     @staticmethod
-    def scratch(rows, cols, wide, far):
-        core, first, second, last = Reduction.sizes(rows, cols, wide, far)
+    def scratch(rows, cols, kind, far, resumed=False):
+        core, first_a, first_b, second, last = Reduction.sizes(rows, cols, kind, far)
+        if resumed:
+            core = first_a = first_b = (16, 128)
         return [
             pltpu.VMEM(core, jnp.bfloat16),
-            pltpu.VMEM((2,) + first, jnp.bfloat16),
-            pltpu.VMEM((2,) + second, jnp.bfloat16),
+            pltpu.VMEM(first_a, jnp.bfloat16),
+            pltpu.VMEM(first_b, jnp.bfloat16),
+            pltpu.VMEM((2,) + ((16, 128) if resumed else second), jnp.bfloat16),
             pltpu.VMEM((2, far) + last, jnp.bfloat16),
             pltpu.VMEM((2,) + last, jnp.bfloat16),
             pltpu.SemaphoreType.DMA((10,)),
@@ -93,33 +96,44 @@
         ]
 
     def view(self, core, part=None, first=None, second=None, piece=None, done=False):
-        sizes = self.sizes(self.rows, self.cols, self.wide, self.grid.far)
+        rows, cols = self.rows, self.cols
+        sizes = self.sizes(rows, cols, self.kind, self.grid.far)
         row = col = 0
         shape = sizes[0]
-        if self.wide:
-            col = core * (self.cols // 2)
+        if self.kind == "wide":
+            col = core * (cols // 2)
             if part is not None:
-                col = col + part * (self.cols // 4) + first * (self.cols // 8)
-                shape = sizes[1]
+                col = col + part * (cols // 4) + first * (cols // 8)
             if second is not None:
-                col = col + second * (self.cols // 16)
-                shape = sizes[2]
+                col = col + second * (cols // 16)
+        elif self.kind == "tall":
+            row = core * (rows // 2)
+            if part is not None:
+                col = part * (cols // 2) + first * (cols // 4)
+            if second is not None:
+                row = row + second * (rows // 4)
         else:
-            row = core * (self.rows // 2)
+            row = core * (rows // 2)
             if part is not None:
-                col = part * (self.cols // 2) + first * (self.cols // 4)
-                shape = sizes[1]
-            if second is not None:
-                row = row + second * (self.rows // 4)
-                shape = sizes[2]
+                row = row + part * (rows // 4)
+                y, task = (second, first) if part == 0 else (first, second)
+                row = row if y is None else row + y * (rows // 8)
+                col = 0 if task is None else task * (cols // 2)
+            elif done:
+                col = self.grid.task * (cols // 2)
+                shape = (rows // 2, cols // 2)
+        if part is not None:
+            shape = sizes[1 + part] if second is None else sizes[3]
+        ref = self.result if done else self.work
+        if self.resumed and not done:
+            ref, row, col = self.work.at[part], 0, 0
         if piece is not None:
-            row = row + piece * sizes[3][0]
-            shape = sizes[3]
+            row = row + piece * sizes[4][0]
+            shape = sizes[4]
         if not isinstance(row, int):
             row = pl.multiple_of(row, shape[0] & -shape[0])
         if not isinstance(col, int):
             col = pl.multiple_of(col, 128)
-        ref = self.result if done else self.work
         return ref.at[pl.ds(row, shape[0]), pl.ds(col, shape[1])]
 
     def swap(self, index):
@@ -127,16 +141,16 @@
         part = (index + 1) % 2
         bits = grid.bits(part)
         if index == 0:
-            source, target, device = self.view(1 - grid.core), self.room[0], grid.core_peer
+            source, target, device = self.view(1 - grid.core), self.core_room, grid.core_peer
         elif index < 3:
-            source, target = self.view(grid.core, part, 1 - bits[0]), self.room[1].at[part]
+            source, target = self.view(grid.core, part, 1 - bits[0]), self.first_rooms[part]
             device = grid.peers(part)[0]
         elif index < 5:
-            source, target = self.view(grid.core, part, bits[0], 1 - bits[1]), self.room[2].at[part]
+            source, target = self.view(grid.core, part, bits[0], 1 - bits[1]), self.second_room.at[part]
             device = grid.peers(part)[1]
         elif index < 7:
             source = self.view(grid.core, part, bits[0], bits[1], done=True)
-            target, device = source, grid.peers(part)[1]
+            target, device = source, grid.y_peer if self.kind == "owner" else grid.peers(part)[1]
         elif index < 9:
             source = self.view(grid.core, part, bits[0], done=True)
             target, device = source, grid.peers(part)[0]
@@ -166,9 +180,6 @@
 
         lax.fori_loop(0, rows // step, one, 0)
 
-    def join(self, mine, received):
-        self.add(mine, [mine, received])
-
     def far_copy(self, part, step, back, inward):
         grid = self.grid
         bits = grid.bits(part)
@@ -182,7 +193,7 @@
             slot = lax.rem(grid.high + step, grid.far)
             owner = slot if inward else grid.high
             source = self.view(grid.core, part, bits[0], bits[1], lax.rem(slot, self.pieces))
-            target = self.room[3].at[part, owner]
+            target = self.last_room.at[part, owner]
         line = 2 * part + (1 if back else 0)
         return pltpu.make_async_remote_copy(
             src_ref=source,
@@ -193,67 +204,77 @@
             device_id_type=MESH,
         )
 
-    def far_start(self, back):
-        for part in range(2):
-            for step in range(1, self.pieces if back else self.grid.far):
-                self.far_copy(part, step, back, False).start()
-
-    def far_settle(self, back):
-        for part in range(2):
-            for step in range(1, self.pieces if back else self.grid.far):
-                self.far_copy(part, step, back, True).wait_recv()
-                self.far_copy(part, step, back, False).wait_send()
+    def far_start(self, part, back):
+        for step in range(1, self.pieces if back else self.grid.far):
+            self.far_copy(part, step, back, False).start()
+
+    def far_settle(self, part, back):
+        for step in range(1, self.pieces if back else self.grid.far):
+            self.far_copy(part, step, back, True).wait_recv()
+            self.far_copy(part, step, back, False).wait_send()
 
     def keep(self, part):
         bits = self.grid.bits(part)
         mine = self.view(self.grid.core, part, bits[0], bits[1], self.mine, True)
         return pltpu.make_async_copy(self.done.at[part], mine, self.local.at[part])
 
+    def finish(self, index, part):
+        grid = self.grid
+        bits = grid.bits(part)
+        if index == 0:
+            if part == 0:
+                self.swap(0).wait()
+                mine = self.view(grid.core)
+                self.add(mine, [mine, self.core_room])
+        elif index == 1:
+            self.swap(1 + part).wait()
+            mine = self.view(grid.core, part, bits[0])
+            self.add(mine, [mine, self.first_rooms[part]])
+        elif index == 2:
+            self.swap(3 + part).wait()
+            mine = self.view(grid.core, part, bits[0], bits[1])
+            self.add(mine, [mine, self.second_room.at[part]])
+        elif index == 3:
+            self.far_settle(part, False)
+            self.last_room[part, grid.high] = self.view(grid.core, part, bits[0], bits[1], self.mine)[...]
+            self.add(self.done.at[part], [self.last_room.at[part, slot] for slot in range(grid.far)])
+        elif index == 4:
+            self.far_settle(part, True)
+            self.keep(part).wait()
+        elif index < 7:
+            self.swap(2 * index - 5 + part).wait()
+        elif part == 0:
+            self.swap(9).wait()
+
+    def begin(self, index, part):
+        if index == 0 or index == 7:
+            if part == 0:
+                self.swap(9 if index else 0).start()
+        elif index < 3:
+            self.swap(2 * index - 1 + part).start()
+        elif index == 3:
+            self.far_start(part, False)
+        elif index == 4:
+            self.keep(part).start()
+            self.far_start(part, True)
+        elif index < 7:
+            self.swap(2 * index - 5 + part).start()
+
     def stage(self, index):
-        grid = self.grid
-        if index == 0:
-            self.swap(0).start()
-        elif index == 1:
-            self.swap(0).wait()
-            self.join(self.view(grid.core), self.room[0])
+        owner = self.kind == "owner"
+        if owner and index == 6:
+            return
+        before = 5 if owner and index == 7 else index - 1
+        first = self.resumed and index == 3
+        together = index in (1, 7, 8)
+        for part in range(2):
+            if before >= 0 and not first:
+                self.finish(before, part)
+            if not together:
+                self.begin(index, part)
+        if together:
             for part in range(2):
-                self.swap(1 + part).start()
-        elif index == 2:
-            for part in range(2):
-                self.swap(1 + part).wait()
-                bits = grid.bits(part)
-                self.join(self.view(grid.core, part, bits[0]), self.room[1].at[part])
-                self.swap(3 + part).start()
-        elif index == 3:
-            for part in range(2):
-                self.swap(3 + part).wait()
-                bits = grid.bits(part)
-                self.join(self.view(grid.core, part, bits[0], bits[1]), self.room[2].at[part])
-            self.far_start(False)
-        elif index == 4:
-            self.far_settle(False)
-            for part in range(2):
-                bits = grid.bits(part)
-                mine = self.view(grid.core, part, bits[0], bits[1], self.mine)
-                self.room[3][part, grid.high] = mine[...]
-                self.add(self.done.at[part], [self.room[3].at[part, slot] for slot in range(grid.far)])
-                self.keep(part).start()
-            self.far_start(True)
-        elif index == 5:
-            self.far_settle(True)
-            for part in range(2):
-                self.keep(part).wait()
-                self.swap(5 + part).start()
-        elif index == 6:
-            for part in range(2):
-                self.swap(5 + part).wait()
-                self.swap(7 + part).start()
-        elif index == 7:
-            for part in range(2):
-                self.swap(7 + part).wait()
-            self.swap(9).start()
-        elif index == 8:
-            self.swap(9).wait()
+                self.begin(index, part)
 
 
 class Grid:
@@ -365,19 +386,22 @@
     return total, spread
 
 
-def settle_stats(exchange, stat_ref, vec_ref, out_ref, rows, count, forward, fillers=(None, None)):
+def settle_stats(exchange, stat_ref, vec_refs, out_ref, rows, count, forward, fillers=(None, None)):
     first = jnp.sum(stat_ref[:8], axis=0, keepdims=True)
     second = jnp.sum(stat_ref[8:16], axis=0, keepdims=True)
-    out_ref[:8] = vec_ref[:8]
     if forward:
+        gain, bias = vec_refs[0][...], vec_refs[1][...]
+        out_ref[...] = jnp.zeros_like(out_ref)
+        out_ref[2:3] = gain
+        out_ref[3:4] = bias
         local = first + rows * stat_ref[16:17]
         total, spread = exchange.run(local, second - first * first * (1.0 / rows), rows, True, fillers)
         scale = lax.rsqrt(spread * (1.0 / count) + EPS)
         out_ref[0:1] = total * (1.0 / count)
         out_ref[1:2] = scale
-        out_ref[4:5] = scale * vec_ref[2:3]
-        out_ref[8:] = jnp.zeros_like(out_ref[8:])
+        out_ref[4:5] = scale * gain
     else:
+        out_ref[:8] = vec_refs[0][:8]
         total, spread = exchange.run(first, second, rows, False, fillers)
         out_ref[5:6] = total * (1.0 / count)
         out_ref[6:7] = spread * (1.0 / count)
@@ -389,11 +413,11 @@
 def tail_and_bell(value):
     bell = jnp.exp2(value * value * (-0.5 * LOG2E))
     away = jnp.abs(value)
-    ratio = 1.0 / (1.0 + away * (ERF_P * ROOT_HALF))
-    poly = ERF_A[4]
+    ratio = pltpu.reciprocal(1.0 + away * (ERF_P * ROOT_HALF))
+    poly = 0.5 * ERF_A[4]
     for factor in ERF_A[3::-1]:
-        poly = poly * ratio + factor
-    tail = 0.5 * poly * ratio * bell
+        poly = poly * ratio + 0.5 * factor
+    tail = poly * ratio * bell
     return jnp.where(value >= 0, 1.0 - tail, tail), bell
 
 
@@ -406,8 +430,8 @@
 
 def crown_kernel(
     piece, h_ref, x_ref, thr_ref, cot_hbm, cot_one, cot_two, top_ref, top_one, top_two, vec_ref,
-    out_ref, flow_ref, normed_ref, grad_ref, came_ref, stat_ref, z_ref, acc_ref, sent_ref, sems,
-    cots_ref, cots_peer_ref, top_peer_ref, local_sems, late_sems,
+    out_ref, flow_ref, normed_ref, grad_ref, rest_ref, came_ref, stat_ref, z_ref, acc_ref, sent_ref, sems,
+    cots_ref, cots_peer_ref, top_peer_ref, local_sems, late_sems, twice_ref,
 ):
     step = pl.program_id(0)
     rows, width = x_ref.shape
@@ -453,6 +477,9 @@
 
     span = pl.ds(pl.multiple_of(step * rows, rows), rows)
     cot_ref, cot_peer_ref = cots_ref.at[span], cots_peer_ref.at[span]
+    span = pl.ds(0, rows)
+    twice_ref[0] = cot_ref[...] * jnp.bfloat16(2.0)
+    twice_ref[1] = cot_peer_ref[...] * jnp.bfloat16(2.0)
 
     @pl.when(step == 0)
     def _():
@@ -461,18 +488,15 @@
 
     for start in range(0, width, piece):
         cols = pl.ds(start, piece)
-        g_one = lax.dot_general(
-            cot_ref[...], top_ref[cols], COLS_COLS, preferred_element_type=jnp.float32
-        ).astype(jnp.bfloat16).astype(jnp.float32)
-        g_two = lax.dot_general(
-            cot_peer_ref[...], top_peer_ref[cols], COLS_COLS, preferred_element_type=jnp.float32
-        ).astype(jnp.bfloat16).astype(jnp.float32)
+        g_one = lax.dot_general(twice_ref[0, span], top_ref[cols], COLS_COLS, preferred_element_type=jnp.float32)
+        g_one = g_one.astype(jnp.bfloat16).astype(jnp.float32)
+        g_two = lax.dot_general(twice_ref[1, span], top_peer_ref[cols], COLS_COLS, preferred_element_type=jnp.float32)
+        g_two = g_two.astype(jnp.bfloat16).astype(jnp.float32)
         total = g_one + g_two
         size = jnp.abs(g_one) + jnp.abs(g_two)
-        share = total / jnp.maximum(size, FLOOR)
-        limit = thr_ref[:, cols].astype(jnp.float32)
-        keep = jnp.clip((0.5 / SOFT) * share + ((0.5 / SOFT + 0.5) - limit * (1.0 / SOFT)), 0.0, 1.0)
-        merged = 0.5 * (total - size) + keep * size
+        limit = (thr_ref[:, cols] * jnp.bfloat16(2.0)).astype(jnp.float32)
+        share = total * pltpu.reciprocal(jnp.maximum(size, 2.0 * FLOOR))
+        merged = 0.25 * total + jnp.clip(share + (1.0 - limit), -SOFT, SOFT) * size
         normed = (h_ref[:, cols] - vec_ref[0:1, cols]) * vec_ref[1:2, cols]
         normed_ref[:, cols] = normed.astype(jnp.bfloat16)
         before = normed * vec_ref[2:3, cols] + vec_ref[3:4, cols] + x_ref[:, cols].astype(jnp.float32)
@@ -491,16 +515,35 @@
 
     @pl.when(step == last)
     def _():
-        mine = pl.multiple_of(task * half, half)
-        peer = pl.multiple_of((1 - task) * half, half)
-        grad_ref[:, pl.ds(mine, half)] = acc_ref[:half].T.astype(jnp.bfloat16)
-        grad_ref[:, pl.ds(peer, half)] = acc_ref[half:].T.astype(jnp.bfloat16)
-        send(last).start()
+        rest_ref[...] = sent_ref[pl.ds(last * rows, rows)]
 
     def after():
-        lax.fori_loop(0, last + 1, lambda index, carry: (send(index).wait(), carry)[1], 0)
+        lax.fori_loop(0, last, lambda index, carry: (send(index).wait(), carry)[1], 0)
 
     return after
+
+
+def crown_fill(*refs):
+    used, given, own = refs[:10], refs[10:16], refs[17:]
+    grad_ref, acc_ref = given[3], own[1]
+    half = acc_ref.shape[0] // 2
+    task = lax.axis_index("task")
+
+    def part(index):
+        def run():
+            place = pl.multiple_of((task if index == 0 else 1 - task) * half, half)
+
+            def one(i, carry):
+                cols = pl.ds(pl.multiple_of(i * half, half), half)
+                turned = acc_ref[pl.ds(index * half, half), cols].T
+                grad_ref[cols, pl.ds(place, half)] = turned.astype(jnp.bfloat16)
+                return carry
+
+            lax.fori_loop(0, acc_ref.shape[1] // half, one, 0)
+
+        return run
+
+    return part(0), part(1)
 
 
 def wide(mask, width):
@@ -631,7 +674,7 @@
     )
 
 
-def tiled(kernel, tile, moving, flags, outs, fixed, scratch, name, stats=None, sends=(), far=(), fill=None, turns=()):
+def tiled(kernel, tile, moving, flags, outs, fixed, scratch, name, stats=None, sends=(), far=(), fill=None, turns=(), aside=None):
     tasks = lax.axis_size("task")
     batch = lax.axis_size("batch")
     rows = moving[0].shape[0]
@@ -656,11 +699,11 @@
     ins, made, held = len(operands), len(out_shape), len(scratch)
     run = kernel
     if stats is not None:
-        vec, forward, ident = stats
-        width = vec.shape[1]
+        vecs, forward, ident = stats
+        width = vecs[0].shape[1]
         params.update(collective_id=ident, has_side_effects=True)
-        operands.append(vec)
-        in_specs.append(whole(vec))
+        operands += vecs
+        in_specs += [whole(vec) for vec in vecs]
         out_shape = out_shape + [shape32(16, width)]
         out_specs = out_specs + [whole(out_shape[-1])]
         scratch = scratch + [pltpu.VMEM((24 if forward else 16, width), jnp.float32)]
@@ -672,15 +715,24 @@
             out_specs = out_specs + [hbm]
             scratch = scratch + [pltpu.SemaphoreType.DMA((2,))]
 
+        if aside is not None:
+            operands.append(aside[0])
+            in_specs.append(hbm)
+            out_shape = out_shape + list(aside[1])
+            out_specs = out_specs + [hbm for _ in aside[1]]
+            scratch = scratch + list(aside[2])
+
         def run(*refs):
             refs = list(refs)
             take = lambda n: [refs.pop(0) for _ in range(n)]
             used = take(ins)
-            vec_ref = take(1)[0]
+            vec_refs = take(len(vecs))
             sources = take(len(sends))
+            own_in = take(0 if aside is None else 1)
             given = take(made)
             out_ref = take(1)[0]
             targets = take(len(sends))
+            own_out = take(0 if aside is None else len(aside[1]))
             own = take(held)
             stat_ref = take(1)[0]
             exchange = Exchange(tasks, batch, *take(6))
@@ -695,8 +747,10 @@
 
             def crossing(index):
                 _, view, _, hop = sends[index]
-                return across(view(sources[index]), targets[index], refs[index], hop)
-            if early:
+                return across(view(sources[index]), targets[index], cross_sems[index], hop)
+
+            cross_sems = take(len(sends))
+            if early and aside is None:
 
                 @pl.when(step == 1)
                 def _():
@@ -704,18 +758,31 @@
                     for index in range(len(sends)):
                         crossing(index).start()
 
+            if aside is not None:
+                helper = aside[3](exchange, *own_in, *own_out, *refs)
+                helper.before(step)
+
             after = kernel(*used, *given, stat_ref, *own)
+            if aside is not None:
+                helper.after(step)
+
+                @pl.when(step == 1)
+                def _():
+                    for index in range(len(sends)):
+                        crossing(index).start()
 
             @pl.when(step == last)
             def _():
-                if not early:
+                if not early and aside is None:
                     exchange.met()
                 fillers = (None, None) if fill is None else fill(*used, *given, stat_ref, *own)
-                settle_stats(exchange, stat_ref, vec_ref, out_ref, rows, rows * tasks * batch, forward, fillers)
+                settle_stats(exchange, stat_ref, vec_refs, out_ref, rows, rows * tasks * batch, forward, fillers)
                 for index in range(len(sends)):
                     crossing(index).wait()
                 if after is not None:
                     after()
+                if aside is not None:
+                    helper.end()
 
     return pl.pallas_call(
         run,
@@ -760,13 +827,59 @@
     )
 
 
-def narrow(flow, normed, vec_three, h_two, vec_two, q_two, w_expand, stats, tile):
+class HeadsAside:
+    def __init__(self, batch, shape, last, exchange, source, target, work, *room):
+        self.exchange, self.work, self.target, self.last = exchange, work, target, last
+        self.sum = Reduction(Grid(batch), work, None, *room[:11], "owner")
+        self.load = pltpu.make_async_copy(source, work, room[11].at[0])
+        self.sems = room[11]
+
+    def before(self, step):
+        @pl.when(step == 0)
+        def _():
+            self.load.start()
+
+    def out(self, part):
+        grid = self.sum.grid
+        bits = grid.bits(part)
+        view = self.sum.view(grid.core, part, bits[0], bits[1])
+        return pltpu.make_async_copy(view, self.target.at[part], self.sems.at[1 + part])
+
+    def after(self, step):
+        @pl.when(step == 0)
+        def _():
+            self.exchange.met()
+            self.load.wait()
+            self.sum.stage(0)
+
+        @pl.when(step == 1)
+        def _():
+            self.sum.stage(1)
+
+        @pl.when(step == self.last)
+        def _():
+            self.sum.stage(2)
+
+    def end(self):
+        for part in range(2):
+            self.sum.finish(2, part)
+            self.out(part).start()
+        for part in range(2):
+            self.out(part).wait()
+
+
+def narrow(flow, normed, vec_three, h_two, vec_two, q_two, w_expand, heads, rest, stats, tile):
     rows, mid = h_two.shape
     width = w_expand.shape[1]
+    batch = lax.axis_size("batch")
+    high, across_ = heads.shape
+    scratch = [pltpu.VMEM(heads.shape, jnp.bfloat16)] + Reduction.scratch(high, across_, "owner", batch // LOW)
+    scratch += [pltpu.SemaphoreType.DMA((3,))]
+    helper = functools.partial(HeadsAside, batch, heads.shape, rows // tile - 1)
     return tiled(
         narrow_kernel, tile, [flow, normed, vec_three, h_two, vec_two, q_two, w_expand], [1, 1, 0, 1, 0, 0, 0],
         [shape32(rows, mid)], [shape16(mid, width)], [pltpu.VMEM((rows, width), jnp.bfloat16)], "narrow", stats,
-        fill=narrow_fill,
+        [(rest, lambda ref: ref, rest.shape, "task")], fill=narrow_fill, aside=(heads, [shape16(2, high // 8, across_ // 2)], scratch, helper),
     )
 
 
@@ -776,7 +889,7 @@
     return tiled(
         functools.partial(crown_kernel, piece), tile,
         [h_three, flat_in, limits, cots, *cot_parts, top, *top_parts, vec], [1, 1, 1, 2, 2, 2, 0, 2, 2, 0],
-        [shape32(rows, half), shape16(rows, width), shape16(rows, width)], [shape16(width, 2 * half)],
+        [shape32(rows, half), shape16(rows, width), shape16(rows, width)], [shape16(width, 2 * half), shape16(tile, half)],
         [
             pltpu.VMEM((tile, width), jnp.bfloat16),
             pltpu.VMEM((2 * half, width), jnp.float32),
@@ -787,8 +900,9 @@
             pltpu.VMEM((width, half), jnp.bfloat16),
             pltpu.SemaphoreType.DMA((5,)),
             pltpu.SemaphoreType.DMA((2,)),
+            pltpu.VMEM((2, tile, half), jnp.bfloat16),
         ],
-        "crown", stats, (), [shape16(rows, half)],
+        "crown", stats, (), [shape16(rows, half)], crown_fill,
     )
 
 
@@ -860,22 +974,27 @@
     heads_load, side_load, expand_load, w_load = loads
     keep = pltpu.make_async_copy(dh_ref, out_hbm, whole_sems.at[4])
     heads_load.start()
+    flow_load(0).start()
     for stream in (twos, masks):
         stream.start(0)
-    for index in range(spans):
+    expand_load.start()
+    for index in range(1, spans):
         flow_load(index).start()
-    for load in loads[1:]:
-        load.start()
+    side_load.start()
+    w_load.start()
 
     third = spatial_work.shape[0] // 3
-    works = [(heads_work, heads_out, False), (expand_work, expand_out, True)]
+    works = [(heads_work, heads_out, "owner"), (expand_work, expand_out, "wide")]
     for index in range(3):
         span = pl.ds(index * third, third)
-        works.append((spatial_work.at[span], spatial_out.at[span], False))
+        works.append((spatial_work.at[span], spatial_out.at[span], "tall"))
     for index in range(2):
         span = pl.ds(index * width // 2, width // 2)
-        works.append((reduce_work.at[span], reduce_out.at[span], False))
-    reductions = [Reduction(grid, work, out, *take(10), wide) for work, out, wide in works]
+        works.append((reduce_work.at[span], reduce_out.at[span], "tall"))
+    reductions = []
+    for work, out, kind in works:
+        shape = heads_out.shape if kind == "owner" else None
+        reductions.append(Reduction(grid, work, out, *take(11), kind, shape))
 
     def tick(name):
         for item, stage in AGENDA.get(name, ()):
@@ -904,12 +1023,16 @@
         lane_ref[span, mid : 2 * mid] = dh.astype(low)
         lane_ref[span, :mid] = jnp.concatenate([(dh * above)[SIDE:].astype(low), zero], axis=0)
         lane_ref[span, 2 * mid :] = jnp.concatenate([zero, (dh * below)[: tile - SIDE].astype(low)], axis=0)
+
+        @pl.when(index == 0)
+        def _():
+            expand_load.wait()
+
         ticks("lane", index, 4)
         return carry
 
     exchange.met()
     heads_load.wait()
-    expand_load.wait()
     tick("start")
     lax.fori_loop(0, spans, lanes, 0)
     masks.start(0)
@@ -956,14 +1079,15 @@
 
     lax.fori_loop(0, spans, taps, 0)
     columns.start(0)
-    settle_stats(exchange, stat_ref, vecone_ref, vec_ref, rows, rows * tasks * batch, False)
+    settle_stats(exchange, stat_ref, [vecone_ref], vec_ref, rows, rows * tasks * batch, False)
     tick("xch")
 
     def inner(index, carry):
         span = pl.ds(pl.multiple_of(index * tile, tile), tile)
         dh = norm_grad(flow_ref[span], normed_ref[span].astype(jnp.float32), vec_ref)
-        dh_ref[span] = dh.astype(jnp.bfloat16)
-        dht_ref[:, span] = dh.T.astype(jnp.bfloat16)
+        low = dh.astype(jnp.bfloat16)
+        dh_ref[span] = low
+        dht_ref[:, span] = low.T
         return carry
 
     lax.fori_loop(0, spans, inner, 0)
@@ -983,7 +1107,7 @@
     tick("tail")
 
 
-def back(flow, h_two, vec_two, h_one, vec_one, sides, masks, w_spatial, flat_in, heads, expand, ident, tile):
+def back(flow, h_two, vec_two, h_one, vec_one, sides, masks, w_spatial, flat_in, heads, expand, heads_shape, ident, tile):
     tasks = lax.axis_size("task")
     batch = lax.axis_size("batch")
     far = batch // LOW
@@ -993,8 +1117,8 @@
     cols = 512
     hbm = pl.BlockSpec(memory_space=pl.ANY)
     vmem = pl.BlockSpec(memory_space=pltpu.VMEM)
-    shapes = [(heads.shape, False), (expand.shape, True)] + [((3 * mid, mid), False)] * 3
-    shapes += [((width // 2, mid), False)] * 2
+    shapes = [(heads_shape, "owner"), (expand.shape, "wide")] + [((3 * mid, mid), "tall")] * 3
+    shapes += [((width // 2, mid), "tall")] * 2
     scratch = [
         pltpu.VMEM((2, tile, mid), full),
         pltpu.VMEM((2, tile, 512), low),
@@ -1012,12 +1136,12 @@
         pltpu.SemaphoreType.DMA((5,)),
         pltpu.SemaphoreType.DMA((rows // tile,)),
     ] + Exchange.scratch(tasks, batch, mid)
-    for (high, across_), is_wide in shapes:
-        scratch += Reduction.scratch(high, across_, is_wide, far)
+    for (high, across_), kind in shapes:
+        scratch += Reduction.scratch(high, across_, kind, far, kind == "owner")
     return pl.pallas_call(
         functools.partial(back_kernel, rows, tasks, batch, tile),
         out_shape=[
-            shape16(rows, mid), shape16(*heads.shape), shape16(*expand.shape), shape16(9 * mid, mid),
+            shape16(rows, mid), shape16(*heads_shape), shape16(*expand.shape), shape16(9 * mid, mid),
             shape16(width, mid), shape32(16, mid),
         ],
         in_specs=[hbm] * 9 + [vmem] * 2,
@@ -1031,7 +1155,7 @@
 
 
 def finish_kernel(
-    dh_ref, up_ref, heads_ref, expand_ref, spatial_ref, reduce_ref, mine_ref, came_ref, w_ref, one_ref, two_ref, three_ref,
+    dh_ref, up_ref, heads_ref, expand_ref, spatial_ref, reduce_ref, mine_ref, came_ref, rest_ref, w_ref, one_ref, two_ref, three_ref,
     out_ref, heads_out, expand_out, spatial_out, reduce_out, both_ref, *sums,
 ):
     full = jnp.float32
@@ -1044,7 +1168,8 @@
     spatial_out[...] = spatial_ref[...].astype(full)
     reduce_out[...] = reduce_ref[...].astype(full)
     both_ref[task] = mine_ref[...]
-    both_ref[1 - task] = came_ref[...].astype(full)
+    ends = pl.program_id(0) == pl.num_programs(0) - 1
+    both_ref[1 - task] = jnp.where(ends, rest_ref[...], came_ref[...]).astype(full)
 
     @pl.when(pl.program_id(0) == 0)
     def _():
@@ -1053,7 +1178,9 @@
             sums[2 * index + 1][...] = vec_ref[8:9]
 
 
-def finish(dh, up, heads, expand, spatial, reduce, mine, came, w_reduce, vecs, steps):
+def finish(dh, up, heads, expand, spatial, reduce, mine, came, rest, w_reduce, vecs):
+    steps = mine.shape[0] // rest.shape[0]
+
     def block(array, lead=0):
         zeros = (0,) * (len(array.shape) - 1 - lead)
         height = array.shape[lead] // steps
@@ -1064,7 +1191,7 @@
 
     rows, half = mine.shape
     moving = [dh, up, heads, expand, spatial, reduce, mine, came]
-    fixed = [w_reduce, *vecs]
+    fixed = [rest, w_reduce, *vecs]
     outs = [shape16(*up.shape), shape32(heads.shape[0], half), shape32(*expand.shape), shape32(*spatial.shape), shape32(*reduce.shape)]
     both = shape32(2, rows, half)
     sums = [shape32(1, vec.shape[1]) for vec in vecs for _ in range(2)]
@@ -1105,8 +1232,7 @@
     top_mine = w_heads[0]
 
     def params(gain, bias):
-        zero = jnp.zeros_like(gain)
-        return jnp.stack([zero, zero, gain, bias, zero, zero, zero, zero])
+        return [gain.reshape(1, -1), bias.reshape(1, -1)]
 
     lines = jnp.arange(SIDE, dtype=jnp.int32)
     cuts = crop_cuts.reshape(canvases, 2)
@@ -1141,20 +1267,21 @@
     h_three, q_two, vec_three, top_two, cot_two = widen(
         h_two, vec_two, w_expand, (params(gain_three, bias_three), True, 2), sends, pixels
     )
-    out_mine, flow, normed, grad_heads, out_peer, vec_three = crown(
+    out_mine, flow, normed, grad_heads, rest, out_peer, vec_three = crown(
         h_three, flat_in, threshold.reshape(rows, width), cots, (cot_one, cot_two), top_mine, (top_one, top_two), vec_three,
-        (vec_three, False, 3), pixels, 256,
-    )
-    flow_two, grad_expand, vec_two = narrow(
-        flow, normed, vec_three, h_two, vec_two, q_two, w_expand, (vec_two, False, 4), min(rows, 512)
+        ([vec_three], False, 3), pixels, 256,
+    )
+    heads_shape = grad_heads.shape
+    flow_two, grad_expand, vec_two, rest, grad_heads = narrow(
+        flow, normed, vec_three, h_two, vec_two, q_two, w_expand, grad_heads, rest, ([vec_two], False, 4), min(rows, 512)
     )
     dh_one, grad_heads, grad_expand, grad_spatial, grad_reduce, vec_one = back(
-        flow_two, h_two, vec_two, h_one, vec_one, sides, masks, w_spatial, flat_in, grad_heads, grad_expand, 5,
+        flow_two, h_two, vec_two, h_one, vec_one, sides, masks, w_spatial, flat_in, grad_heads, grad_expand, heads_shape, 5,
         min(rows, 512),
     )
     grad_inputs, grad_heads, grad_expand, grad_spatial, grad_reduce, head_out, *sums = finish(
-        dh_one, flow, grad_heads, grad_expand, grad_spatial, grad_reduce, out_mine, out_peer, w_reduce,
-        (vec_one, vec_two, vec_three), 8,
+        dh_one, flow, grad_heads, grad_expand, grad_spatial, grad_reduce, out_mine, out_peer, rest, w_reduce,
+        (vec_one, vec_two, vec_three),
     )
     return (
         head_out.reshape(1, 2, canvases, pixels, half),

time: 303 us -> 293 us (0.967)
  Pallas kernels: 294 us -> 287 us
    pallas_call x1, Pallas kernels: 117 us -> 106 us  [back(): pl.pallas_call(functools.partial(back_kernel, rows, tasks, batch, tile),...]
    pallas_call x5, Pallas kernels: 154 us -> 158 us  [tiled(): pl.pallas_call(run, grid=(rows // tile,), out_shape=out_shape, in_specs=i...]
where the time goes in v2:
time: 293 us; the launch traced here: 292 us
  Pallas kernels  287 us (98%)
    pallas_call x5, Pallas kernels, tiled(): pl.pallas_call(run, grid=(rows // tile,), out_shape=out_shape, in_specs=i...  158 us
    pallas_call x1, Pallas kernels, back(): pl.pallas_call(functools.partial(back_kernel, rows, tasks, batch, tile),...  106 us
    pallas_call x1, Pallas kernels, finish(): pl.pallas_call(finish_kernel, grid=(steps,), out_shape=outs + [both] + su...  22.5 us

profile of v2, /device:TPU:0, one launch (start us, length us, event | category | flops | bytes accessed | tf_op | source)
XLA Modules:
  0.0 292.5 jit_solution(2880446171157892468)
XLA Ops:
  0.7 0.8 slice_bitcast_fusion.1
  1.4 0.1 fusion.1
  1.5 0.1 slice.15
  1.6 0.1 slice.18
  1.7 0.1 broadcast_in_dim.56
  1.8 0.1 broadcast_in_dim.57
  1.9 0.1 broadcast_in_dim.53
  1.9 0.1 broadcast_in_dim.54
  2.1 0.1 broadcast_in_dim.51
  2.2 0.1 broadcast_in_dim.48
  2.3 0.3 broadcast_in_dim.49
  2.6 0.3 broadcast_in_dim.52
  3.0 0.3 broadcast_in_dim.55
  3.3 0.3 broadcast_in_dim.58
  3.6 2.0 add_convert_fusion.refs_2_.refs_4_
  5.7 20.9 %squeeze.5 = (f32[2048,512]{1,0:T(8,128)}, f32[16,512]{1,0:T(8,128)}) custom-call(bf16[2048,2048]{1,0:T(8,128)(2,1)} %bitcast.26, bf16[2048,512]{1,0:T(8,128)(2,1)} %w_ref.1, f32[1,512]{1,0:T(1,128)} %bitcast.38, f32[1,512]{1,0:T(1,128)} %bitcast.39), custom_call_target="tpu_custom_call" | custom-call | tf_op jit(solution)/shard_map/squeeze/pallas_call | solution.py:787
  26.5 28.1 %mesh_forward.1 = (f32[2048,512]{1,0:T(8,128)}, bf16[1536,2048]{1,0:T(8,128)(2,1)}, f32[16,512]{1,0:T(8,128)}, bf16[1024,256]{1,0:T(8,128)(2,1)}, bf16[512,256]{1,0:T(8,128)(2,1)}) custom-call(f32[2048,512]{1,0:T(8,128)} %get-tuple-element.54.refs_0_.refs_2_, f32[16,512]{1,0:T(8,128)} %get-tuple-element.55.refs_1_.refs_10_, ...), custom_call_target="tpu_custom_call" | custom-call | tf_op jit(solution)/shard_map/mesh_forward/pallas_call | solution.py:787
  54.7 23.9 %widen.1 = (f32[2048,2048]{1,0:T(8,128)}, bf16[512,2048]{1,0:T(8,128)(2,1)}, f32[16,2048]{1,0:T(8,128)}, bf16[1024,256]{1,0:T(8,128)(2,1)}, bf16[512,256]{1,0:T(8,128)(2,1)}) custom-call(f32[2048,512]{1,0:T(8,128)} %get-tuple-element.56.refs_0_.refs_3_.refs_1_, f32[16,512]{1,0:T(8,128)} %get-tuple-element.57.refs_1_.refs_4_.refs_7_, ...), custom_call_target="tpu_custom_call" | custom-call | tf_op jit(solution)/shard_map/widen/pallas_call | solution.py:787
  78.6 53.3 %crown.1 = (f32[2048,256]{1,0:T(8,128)}, bf16[2048,2048]{1,0:T(8,128)(2,1)}, bf16[2048,2048]{1,0:T(8,128)(2,1)}, bf16[2048,512]{1,0:T(8,128)(2,1)}, bf16[256,256...) custom-call(f32[2048,2048]{1,0:T(8,128)} %get-tuple-element.59.refs_0_, bf16[2048,2048]{1,0:T(8,128)(2,1)} %bitcast.27, ...), custom_call_target="tpu_custom_call" | custom-call | tf_op jit(solution)/shard_map/crown/pallas_call | solution.py:787
  131.9 31.8 %narrow.1 = (f32[2048,512]{1,0:T(8,128)}, bf16[512,2048]{1,0:T(8,128)(2,1)}, f32[16,512]{1,0:T(8,128)}, bf16[256,256]{1,0:T(8,128)(2,1)}, bf16[2,256,256]{2,1,0:T(8,128)(2,1)}) custom-call(bf16[2048,2048]{1,0:T(8,128)(2,1)} %get-tuple-element.64.refs_0_.up_ref, bf16[2048,2048]{1,0:T(8,128)(2,1)} %get-tuple-element.65.refs_1_, ...), custom_call_target="tpu_custom_call" | custom-call | tf_op jit(solution)/shard_map/narrow/pallas_call | solution.py:787
  163.7 106.1 %back.1 = (bf16[2048,512]{1,0:T(8,128)(2,1)}, bf16[2048,512]{1,0:T(8,128)(2,1)}, bf16[512,2048]{1,0:T(8,128)(2,1)}, bf16[4608,512]{1,0:T(8,128)(2,1)}, bf16[2048,512]{1,0:T(8,128)(2,1)}, /*index=5*/f32[16,512]{1,0:T(8,128)}) custom-call(f32[2048,512]{1,0:T(8,128)} %get-tuple-element.70.refs_0_, f32[2048,512]{1,0:T(8,128)} %get-tuple-element.56.refs_0_.refs_3_.refs_1_, ...), custom_call_target="tpu_custom_call" | custom-call | tf_op jit(solution)/shard_map/back/pallas_call | solution.py:1141
  269.8 22.5 %finish.1 = (bf16[2048,2048]{1,0:T(8,128)(2,1)}, f32[2048,256]{1,0:T(8,128)}, f32[512,2048]{1,0:T(8,128)}, f32[4608,512]{1,0:T(8,128)}, f32[2048,512]{1,0:T(8,12...) custom-call(bf16[2048,512]{1,0:T(8,128)(2,1)} %get-tuple-element.75., ...), custom_call_target="tpu_custom_call" | custom-call | tf_op jit(solution)/shard_map/finish/pallas_call | solution.py:1198
  (5 shorter events, 0.0 us)

commit v3 on v2

--- a/solution.py
+++ b/solution.py
@@ -314,8 +314,8 @@
     def scratch(tasks, batch, width):
         near_size, far_size = tasks * LOW, batch // LOW
         return [
-            pltpu.VMEM((near_size + 1, 2, width), jnp.float32),
-            pltpu.VMEM((far_size + 1, 2, width), jnp.float32),
+            pltpu.VMEM((near_size + 1, 2 * width // 128, 128), jnp.float32),
+            pltpu.VMEM((far_size + 1, 2 * width // 128, 128), jnp.float32),
             pltpu.SemaphoreType.DMA((near_size,)),
             pltpu.SemaphoreType.DMA((near_size,)),
             pltpu.SemaphoreType.DMA((far_size,)),
@@ -362,27 +362,36 @@
             copy(step, peer(step)[0]).wait_recv()
         for step in range(1, size):
             copy(step, me).wait_send()
-        return held[:size]
+        return held.at[pl.ds(0, size)]
 
     def run(self, total, spread, rows, forward, fillers=(None, None)):
-        self.near[self.near_size, 0:1] = total
-        self.near[self.near_size, 1:2] = spread
+        lines = total.shape[1] // 128
+        for line in range(lines):
+            cols = slice(line * 128, (line + 1) * 128)
+            self.near[self.near_size, line : line + 1] = total[:, cols]
+            self.near[self.near_size, lines + line : lines + line + 1] = spread[:, cols]
         held = self.hop(self.near_size, self.near_peer, self.me_near, self.near, self.near_sems, fillers[0])
         total, spread = join(held, float(rows), forward)
-        self.far[self.far_size, 0:1] = total
-        self.far[self.far_size, 1:2] = spread
+        self.far[self.far_size, :lines] = total
+        self.far[self.far_size, lines:] = spread
         held = self.hop(self.far_size, self.far_peer, self.high, self.far, self.far_sems, fillers[1])
-        return join(held, float(rows * self.near_size), forward)
+        total, spread = join(held, float(rows * self.near_size), forward)
+        flat = lambda array: jnp.concatenate([array[line : line + 1] for line in range(lines)], axis=1)
+        return flat(total), flat(spread)
 
 
 def join(held, share, forward):
-    sums = held[:, 0, :]
-    total = jnp.sum(sums, axis=0, keepdims=True)
-    spread = jnp.sum(held[:, 1, :], axis=0, keepdims=True)
+    groups, lines = held.shape[0], held.shape[1] // 2
+    total = held[0, :lines]
+    spread = held[0, lines:]
+    for group in range(1, groups):
+        total = total + held[group, :lines]
+        spread = spread + held[group, lines:]
     if forward:
-        groups = held.shape[0]
-        away = sums * (1.0 / share) - total * (1.0 / (share * groups))
-        spread = spread + share * jnp.sum(away * away, axis=0, keepdims=True)
+        centre = total * (1.0 / (share * groups))
+        for group in range(groups):
+            away = held[group, :lines] * (1.0 / share) - centre
+            spread = spread + share * (away * away)
     return total, spread
 
 
@@ -550,6 +559,24 @@
     return jnp.concatenate([mask] * (width // mask.shape[1]), axis=1)
 
 
+def edges(cuts_ref, canvas):
+    shape = (SIDE * SIDE, 128)
+    pixel = lax.broadcasted_iota(jnp.int32, shape, 0)
+    row, col = pixel // SIDE, lax.rem(pixel, SIDE)
+    down, right = cuts_ref[canvas, 0], cuts_ref[canvas, 1]
+    one, zero = jnp.ones(shape, jnp.float32), jnp.zeros(shape, jnp.float32)
+    within = lambda place, rim, cut: jnp.where((place != rim) & (place != cut), one, zero)
+    return (
+        within(col, 0, right), within(col, SIDE - 1, right - 1), within(row, 0, down), within(row, SIDE - 1, down - 1),
+    )
+
+
+def edges_of(cuts_ref, step, rows):
+    count = rows // (SIDE * SIDE)
+    parts = [edges(cuts_ref, step * count + index) for index in range(count)]
+    return [jnp.concatenate([part[side] for part in parts], axis=0) for side in range(4)]
+
+
 def gather_stats(stat_ref, hidden, first):
     @pl.when(first)
     def _():
@@ -572,15 +599,15 @@
     gather_stats(stat_ref, hidden, pl.program_id(0) == 0)
 
 
-def mesh_kernel(h_ref, vec_ref, mask_ref, w_ref, out_ref, side_ref, stat_ref, pad_ref):
+def mesh_kernel(h_ref, vec_ref, cuts_ref, w_ref, out_ref, side_ref, stat_ref, pad_ref):
     rows, mid = h_ref.shape
     inner = pl.ds(SIDE, rows)
     before = normal(h_ref[...], vec_ref) * vec_ref[2:3] + vec_ref[3:4]
     phi, _ = tail_and_bell(before)
     low = (before * phi).astype(jnp.bfloat16)
     kept = low.astype(jnp.float32)
-    left = wide(mask_ref[:, :128].astype(jnp.float32), mid)
-    right = wide(mask_ref[:, 128:256].astype(jnp.float32), mid)
+    left, right, above, below = edges_of(cuts_ref, pl.program_id(0), rows)
+    left, right = wide(left, mid), wide(right, mid)
 
     @pl.when(pl.program_id(0) == 0)
     def _():
@@ -591,8 +618,8 @@
     pad_ref[inner, mid : 2 * mid] = low
     pad_ref[inner, 2 * mid :] = (pltpu.roll(kept, rows - 1, 0) * right).astype(jnp.bfloat16)
     side_ref[...] = pad_ref[inner].T
-    above = wide(mask_ref[:, 256:384], 3 * mid)
-    below = wide(mask_ref[:, 384:], 3 * mid)
+    above = wide(above.astype(jnp.bfloat16), 3 * mid)
+    below = wide(below.astype(jnp.bfloat16), 3 * mid)
     hidden = jnp.dot(pad_ref[inner], w_ref[3 * mid : 6 * mid], preferred_element_type=jnp.float32)
     hidden += jnp.dot(pad_ref[:rows] * above, w_ref[: 3 * mid], preferred_element_type=jnp.float32)
     hidden += jnp.dot(pad_ref[2 * SIDE :] * below, w_ref[6 * mid :], preferred_element_type=jnp.float32)
@@ -691,7 +718,7 @@
 
     hbm = pl.BlockSpec(memory_space=pl.ANY)
     operands = list(moving)
-    in_specs = [(whole, block, lambda a: hbm)[m](a) for a, m in zip(moving, flags)]
+    in_specs = [(whole, block, lambda a: hbm, lambda a: pl.BlockSpec(memory_space=pltpu.SMEM))[m](a) for a, m in zip(moving, flags)]
     out_shape = outs + fixed + list(far)
     out_specs = [turned(a) if i in turns else block(a) for i, a in enumerate(outs)] + [whole(a) for a in fixed] + [hbm for a in far]
     scratch = list(scratch)
@@ -809,10 +836,10 @@
     return tiled(squeeze_kernel, tile, [flat_in, w_reduce], [1, 0], [shape32(rows, mid)], [], [], "squeeze", stats)
 
 
-def mesh_forward(h_one, vec, masks, taps, stats, sends, tile):
+def mesh_forward(h_one, vec, cuts, taps, stats, sends, tile):
     rows, mid = h_one.shape
     return tiled(
-        mesh_kernel, tile, [h_one, vec, masks, taps], [1, 0, 1, 0],
+        mesh_kernel, tile, [h_one, vec, cuts, taps], [1, 0, 3, 0],
         [shape32(rows, mid), shape16(3 * mid, rows)], [],
         [pltpu.VMEM((tile + 2 * SIDE, 3 * mid), jnp.bfloat16)], "mesh_forward", stats, sends, turns=(1,),
     )
@@ -933,10 +960,10 @@
     def take(count):
         return [refs.pop(0) for _ in range(count)]
 
-    (flow_hbm, two_hbm, one_hbm, side_hbm, mask_hbm, w_hbm, x_hbm, heads_hbm, expand_hbm) = take(9)
-    vectwo_ref, vecone_ref = take(2)
+    (flow_hbm, two_hbm, one_hbm, side_hbm, w_hbm, x_hbm, heads_hbm, expand_hbm) = take(8)
+    vectwo_ref, vecone_ref, cuts_ref = take(3)
     (out_hbm, heads_out, expand_out, spatial_out, reduce_out, vec_ref) = take(6)
-    (two_buf, mask_buf, x_buf) = take(3)
+    (two_buf, x_buf) = take(2)
     (side_ref, lane_ref, flow_ref, w_ref) = take(4)
     heads_work, expand_work, spatial_work, reduce_work, stat_ref = take(5)
     pair_sems, whole_sems, flow_sems = take(3)
@@ -957,7 +984,6 @@
         )
 
     twos = Stream(blocks(two_hbm, tile), two_buf, pair_sems.at[1])
-    masks = Stream(blocks(mask_hbm, tile), mask_buf, pair_sems.at[2])
     ones = Stream(blocks(one_hbm, tile), two_buf, pair_sems.at[3])
     dh_ref, normed_ref, dht_ref = lane_ref.at[:, :mid], lane_ref.at[:, mid : 2 * mid], side_ref.at[:mid]
     across_cols = x_buf.shape[2]
@@ -975,8 +1001,7 @@
     keep = pltpu.make_async_copy(dh_ref, out_hbm, whole_sems.at[4])
     heads_load.start()
     flow_load(0).start()
-    for stream in (twos, masks):
-        stream.start(0)
+    twos.start(0)
     expand_load.start()
     for index in range(1, spans):
         flow_load(index).start()
@@ -1014,10 +1039,9 @@
         flow_load(index).wait()
         flow = flow_ref[span]
         normed = normal(twos.take(index, spans)[...], vectwo_ref)
-        mask = masks.take(index, spans)
         dh = norm_grad(flow, normed, vectwo_ref)
-        above = wide(mask[:, 256:384].astype(jnp.float32), mid)
-        below = wide(mask[:, 384:].astype(jnp.float32), mid)
+        _, _, above, below = edges_of(cuts_ref, index, tile)
+        above, below = wide(above, mid), wide(below, mid)
         low = jnp.bfloat16
         zero = jnp.zeros((SIDE, mid), low)
         lane_ref[span, mid : 2 * mid] = dh.astype(low)
@@ -1035,7 +1059,6 @@
     heads_load.wait()
     tick("start")
     lax.fori_loop(0, spans, lanes, 0)
-    masks.start(0)
     ones.start(0)
     side_load.wait()
 
@@ -1053,7 +1076,6 @@
 
     def taps(index, carry):
         span = pl.ds(pl.multiple_of(index * tile, tile), tile)
-        mask = masks.take(index, spans)
         pieces = []
         for b in range(3):
             total = None
@@ -1066,8 +1088,8 @@
             pieces.append(total)
             if b < 2:
                 ticks("tap", index, 4, 3, b)
-        left = wide(mask[:, :128].astype(jnp.float32), mid)
-        right = wide(mask[:, 128:256].astype(jnp.float32), mid)
+        left, right, _, _ = edges_of(cuts_ref, index, tile)
+        left, right = wide(left, mid), wide(right, mid)
         dq = pieces[1] + pltpu.roll(pieces[0] * left, tile - 1, 0) + pltpu.roll(pieces[2] * right, 1, 0)
         normed = normal(ones.take(index, spans)[...], vecone_ref)
         flow = dq * act_slope(normed * vecone_ref[2:3] + vecone_ref[3:4])
@@ -1107,7 +1129,7 @@
     tick("tail")
 
 
-def back(flow, h_two, vec_two, h_one, vec_one, sides, masks, w_spatial, flat_in, heads, expand, heads_shape, ident, tile):
+def back(flow, h_two, vec_two, h_one, vec_one, sides, cuts, w_spatial, flat_in, heads, expand, heads_shape, ident, tile):
     tasks = lax.axis_size("task")
     batch = lax.axis_size("batch")
     far = batch // LOW
@@ -1121,7 +1143,6 @@
     shapes += [((width // 2, mid), "tall")] * 2
     scratch = [
         pltpu.VMEM((2, tile, mid), full),
-        pltpu.VMEM((2, tile, 512), low),
         pltpu.VMEM((2, rows, cols), low),
         pltpu.VMEM((3 * mid, rows), low),
         pltpu.VMEM((rows, 3 * mid), low),
@@ -1144,14 +1165,14 @@
             shape16(rows, mid), shape16(*heads_shape), shape16(*expand.shape), shape16(9 * mid, mid),
             shape16(width, mid), shape32(16, mid),
         ],
-        in_specs=[hbm] * 9 + [vmem] * 2,
+        in_specs=[hbm] * 8 + [vmem] * 2 + [pl.BlockSpec(memory_space=pltpu.SMEM)],
         out_specs=[hbm] * 5 + [vmem],
         scratch_shapes=scratch,
         compiler_params=pltpu.CompilerParams(
             vmem_limit_bytes=VMEM_BYTES, collective_id=ident, has_side_effects=True
         ),
         name="back",
-    )(flow, h_two, h_one, sides, masks, w_spatial, flat_in, heads, expand, vec_two, vec_one)
+    )(flow, h_two, h_one, sides, w_spatial, flat_in, heads, expand, vec_two, vec_one, cuts)
 
 
 def finish_kernel(
@@ -1168,8 +1189,13 @@
     spatial_out[...] = spatial_ref[...].astype(full)
     reduce_out[...] = reduce_ref[...].astype(full)
     both_ref[task] = mine_ref[...]
-    ends = pl.program_id(0) == pl.num_programs(0) - 1
-    both_ref[1 - task] = jnp.where(ends, rest_ref[...], came_ref[...]).astype(full)
+    both_ref[1 - task] = came_ref[...].astype(full)
+
+    @pl.when(pl.program_id(0) == pl.num_programs(0) - 1)
+    def _():
+        height = rest_ref.shape[0]
+        both_ref[1 - task, both_ref.shape[1] - height :] = rest_ref[...].astype(full)
+
 
     @pl.when(pl.program_id(0) == 0)
     def _():
@@ -1178,8 +1204,7 @@
             sums[2 * index + 1][...] = vec_ref[8:9]
 
 
-def finish(dh, up, heads, expand, spatial, reduce, mine, came, rest, w_reduce, vecs):
-    steps = mine.shape[0] // rest.shape[0]
+def finish(dh, up, heads, expand, spatial, reduce, mine, came, rest, w_reduce, vecs, steps):
 
     def block(array, lead=0):
         zeros = (0,) * (len(array.shape) - 1 - lead)
@@ -1222,8 +1247,6 @@
     bias_three,
     cotangent,
 ):
-    low = jnp.bfloat16
-    full = jnp.float32
     canvases, pixels, width = inputs.shape[1:]
     mid = w_reduce.shape[1]
     rows = canvases * pixels
@@ -1234,19 +1257,7 @@
     def params(gain, bias):
         return [gain.reshape(1, -1), bias.reshape(1, -1)]
 
-    lines = jnp.arange(SIDE, dtype=jnp.int32)
     cuts = crop_cuts.reshape(canvases, 2)
-    from_above = jnp.logical_not((lines == cuts[:, 0:1]) | (lines == 0)[None, :])
-    from_left = jnp.logical_not((lines == cuts[:, 1:2]) | (lines == 0)[None, :])
-    from_below = jnp.pad(from_above[:, 1:], ((0, 0), (0, 1)))
-    from_right = jnp.pad(from_left[:, 1:], ((0, 0), (0, 1)))
-    shape = (canvases, SIDE, SIDE, 128)
-    masks = jnp.concatenate(
-        [jnp.broadcast_to(m[:, None, :, None], shape) for m in (from_left, from_right)]
-        + [jnp.broadcast_to(m[:, :, None, None], shape) for m in (from_above, from_below)],
-        axis=3,
-    ).astype(low).reshape(rows, 512)
-
     flat_in = inputs.reshape(rows, width)
     core = lambda: lax.rem(lax.axis_index("batch"), 2)
     other = lambda: 1 - lax.axis_index("task")
@@ -1258,7 +1269,7 @@
         (cots, lambda ref: ref.at[other(), pl.ds(0, quarter)], (quarter, half), "task"),
     ]
     h_two, sides, vec_two, top_one, cot_one = mesh_forward(
-        h_one, vec_one, masks, w_spatial.reshape(9 * mid, mid), (params(gain_two, bias_two), True, 1), sends, pixels
+        h_one, vec_one, cuts, w_spatial.reshape(9 * mid, mid), (params(gain_two, bias_two), True, 1), sends, pixels
     )
     sends = [
         (top_one, lambda ref: ref, (top_rows, half), "core"),
@@ -1276,12 +1287,12 @@
         flow, normed, vec_three, h_two, vec_two, q_two, w_expand, grad_heads, rest, ([vec_two], False, 4), min(rows, 512)
     )
     dh_one, grad_heads, grad_expand, grad_spatial, grad_reduce, vec_one = back(
-        flow_two, h_two, vec_two, h_one, vec_one, sides, masks, w_spatial, flat_in, grad_heads, grad_expand, heads_shape, 5,
+        flow_two, h_two, vec_two, h_one, vec_one, sides, cuts, w_spatial, flat_in, grad_heads, grad_expand, heads_shape, 5,
         min(rows, 512),
     )
     grad_inputs, grad_heads, grad_expand, grad_spatial, grad_reduce, head_out, *sums = finish(
         dh_one, flow, grad_heads, grad_expand, grad_spatial, grad_reduce, out_mine, out_peer, rest, w_reduce,
-        (vec_one, vec_two, vec_three),
+        (vec_one, vec_two, vec_three), 2,
     )
     return (
         head_out.reshape(1, 2, canvases, pixels, half),

time: 293 us -> 289 us (0.986)
  no operation moved by 1% of the time
where the time goes in v3:
time: 289 us; the launch traced here: 288 us
  Pallas kernels  286 us (99%)
    pallas_call x5, Pallas kernels, tiled(): pl.pallas_call(run, grid=(rows // tile,), out_shape=out_shape, in_specs=i...  158 us
    pallas_call x1, Pallas kernels, back(): pl.pallas_call(functools.partial(back_kernel, rows, tasks, batch, tile),...  108 us
    pallas_call x1, Pallas kernels, finish(): pl.pallas_call(finish_kernel, grid=(steps,), out_shape=outs + [both] + su...  20.6 us

profile of v3, /device:TPU:0, one launch (start us, length us, event | category | flops | bytes accessed | tf_op | source)
XLA Modules:
  0.0 288.3 jit_solution(15787004395290435257)
XLA Ops:
  0.6 1.3 copy.26.refs_2_.refs_10_
  2.0 20.8 %squeeze.5 = (f32[2048,512]{1,0:T(8,128)}, f32[16,512]{1,0:T(8,128)}) custom-call(bf16[2048,2048]{1,0:T(8,128)(2,1)} %bitcast.22, bf16[2048,512]{1,0:T(8,128)(2,1)} %w_ref.1, f32[1,512]{1,0:T(1,128)} %bitcast.34, f32[1,512]{1,0:T(1,128)} %bitcast.35), custom_call_target="tpu_custom_call" | custom-call | tf_op jit(solution)/shard_map/squeeze/pallas_call | solution.py:814
  22.8 28.5 %mesh_forward.1 = (f32[2048,512]{1,0:T(8,128)}, bf16[1536,2048]{1,0:T(8,128)(2,1)}, f32[16,512]{1,0:T(8,128)}, bf16[1024,256]{1,0:T(8,128)(2,1)}, bf16[512,256]{1,0:T(8,128)(2,1)}) custom-call(f32[2048,512]{1,0:T(8,128)} %get-tuple-element.54.refs_0_.refs_2_, f32[16,512]{1,0:T(8,128)} %get-tuple-element.55.refs_1_.refs_9_, s32[8,2]{1,0:T(8,128)} %copy.26.refs_2_.refs_10_, ...), custom_call_target="tpu_custom_call" | custom-call | tf_op jit(solution)/shard_map/mesh_forward/pallas_call | solution.py:814
  51.3 23.7 %widen.1 = (f32[2048,2048]{1,0:T(8,128)}, bf16[512,2048]{1,0:T(8,128)(2,1)}, f32[16,2048]{1,0:T(8,128)}, bf16[1024,256]{1,0:T(8,128)(2,1)}, bf16[512,256]{1,0:T(8,128)(2,1)}) custom-call(f32[2048,512]{1,0:T(8,128)} %get-tuple-element.56.refs_0_.refs_3_.refs_1_, f32[16,512]{1,0:T(8,128)} %get-tuple-element.57.refs_1_.refs_4_.refs_7_, ...), custom_call_target="tpu_custom_call" | custom-call | tf_op jit(solution)/shard_map/widen/pallas_call | solution.py:814
  75.0 53.2 %crown.1 = (f32[2048,256]{1,0:T(8,128)}, bf16[2048,2048]{1,0:T(8,128)(2,1)}, bf16[2048,2048]{1,0:T(8,128)(2,1)}, bf16[2048,512]{1,0:T(8,128)(2,1)}, bf16[256,256...) custom-call(f32[2048,2048]{1,0:T(8,128)} %get-tuple-element.59.refs_0_, bf16[2048,2048]{1,0:T(8,128)(2,1)} %bitcast.23, ...), custom_call_target="tpu_custom_call" | custom-call | tf_op jit(solution)/shard_map/crown/pallas_call | solution.py:814
  128.2 31.7 %narrow.1 = (f32[2048,512]{1,0:T(8,128)}, bf16[512,2048]{1,0:T(8,128)(2,1)}, f32[16,512]{1,0:T(8,128)}, bf16[256,256]{1,0:T(8,128)(2,1)}, bf16[2,256,256]{2,1,0:T(8,128)(2,1)}) custom-call(bf16[2048,2048]{1,0:T(8,128)(2,1)} %get-tuple-element.64.refs_0_.up_ref, bf16[2048,2048]{1,0:T(8,128)(2,1)} %get-tuple-element.65.refs_1_, ...), custom_call_target="tpu_custom_call" | custom-call | tf_op jit(solution)/shard_map/narrow/pallas_call | solution.py:814
  160.0 107.5 %back.1 = (bf16[2048,512]{1,0:T(8,128)(2,1)}, bf16[2048,512]{1,0:T(8,128)(2,1)}, bf16[512,2048]{1,0:T(8,128)(2,1)}, bf16[4608,512]{1,0:T(8,128)(2,1)}, bf16[2048,512]{1,0:T(8,128)(2,1)}, /*index=5*/f32[16,512]{1,0:T(8,128)}) custom-call(f32[2048,512]{1,0:T(8,128)} %get-tuple-element.70.refs_0_, f32[2048,512]{1,0:T(8,128)} %get-tuple-element.56.refs_0_.refs_3_.refs_1_, ...), custom_call_target="tpu_custom_call" | custom-call | tf_op jit(solution)/shard_map/back/pallas_call | solution.py:1162
  267.5 20.6 %finish.1 = (bf16[2048,2048]{1,0:T(8,128)(2,1)}, f32[2048,256]{1,0:T(8,128)}, f32[512,2048]{1,0:T(8,128)}, f32[4608,512]{1,0:T(8,128)}, f32[2048,512]{1,0:T(8,12...) custom-call(bf16[2048,512]{1,0:T(8,128)(2,1)} %get-tuple-element.75., ...), custom_call_target="tpu_custom_call" | custom-call | tf_op jit(solution)/shard_map/finish/pallas_call | solution.py:1223

commit v4 on v3

--- a/solution.py
+++ b/solution.py
@@ -33,15 +33,16 @@
     "sp4": ((1, 2), (2, 1),),
     "sp5": ((3, 0),),
     "sp8": ((0, 5), (1, 3), (3, 1), (4, 0),),
-    "tap1": ((2, 2), (4, 1),),
+    "tap2": ((2, 2), (4, 1),),
     "tap5": ((0, 7), (1, 4),),
-    "tap7": ((0, 8), (3, 2),),
-    "tap8": ((2, 3),),
-    "xch": ((1, 5), (2, 4), (3, 3), (4, 2),),
-    "inner": ((1, 6),),
-    "red1": ((2, 5), (4, 3), (5, 0),),
-    "red3": ((3, 4), (5, 1), (6, 0), (1, 7),),
-    "tail": ((2, 6), (6, 1), (4, 4), (1, 8), (5, 2), (3, 5), (2, 7), (2, 8), (6, 2), (4, 5), (5, 3), (3, 6), (6, 3), (4, 6), (5, 4), (3, 7), (6, 4), (3, 8), (5, 5), (4, 7), (6, 5), (5, 6), (4, 8), (6, 6), (5, 7), (5, 8), (6, 7), (6, 8),),
+    "tap8": ((0, 8), (3, 2), (2, 3),),
+    "xb": ((1, 5), (2, 4), (3, 3), (4, 2),),
+    "xch": ((1, 6),),
+    "inner": ((2, 5), (4, 3),),
+    "red1": ((1, 7), (3, 4), (5, 0),),
+    "red2": ((2, 6),),
+    "red3": ((1, 8), (4, 4), (5, 1), (6, 0),),
+    "tail": ((6, 1), (3, 5), (2, 7), (2, 8), (5, 2), (4, 5), (6, 2), (3, 6), (5, 3), (4, 6), (6, 3), (5, 4), (3, 7), (6, 4), (3, 8), (4, 7), (5, 5), (4, 8), (6, 5), (5, 6), (6, 6), (5, 7), (5, 8), (6, 7), (6, 8),),
 }
 
 
@@ -578,7 +579,7 @@
 
 
 def gather_stats(stat_ref, hidden, first):
-    @pl.when(first)
+    @pl.when(False if first is None else first)
     def _():
         stat_ref[:16] = jnp.zeros_like(stat_ref[:16])
         mean = jnp.sum(hidden, axis=0, keepdims=True) / hidden.shape[0]
@@ -628,13 +629,19 @@
 
 
 def widen_kernel(h_ref, vec_ref, w_ref, out_ref, low_ref, stat_ref):
-    before = normal(h_ref[...], vec_ref) * vec_ref[2:3] + vec_ref[3:4]
-    phi, _ = tail_and_bell(before)
-    low = (before * phi).astype(jnp.bfloat16)
-    low_ref[...] = low.T
-    hidden = jnp.dot(low, w_ref[...], preferred_element_type=jnp.float32)
-    out_ref[...] = hidden
-    gather_stats(stat_ref, hidden, pl.program_id(0) == 0)
+    rows = h_ref.shape[0]
+    spans = [pl.ds(start, rows // 2) for start in (0, rows // 2)]
+    lows = []
+    for span in spans:
+        before = normal(h_ref[span], vec_ref) * vec_ref[2:3] + vec_ref[3:4]
+        phi, _ = tail_and_bell(before)
+        low = (before * phi).astype(jnp.bfloat16)
+        low_ref[:, span] = low.T
+        lows.append(low)
+    for index, span in enumerate(spans):
+        hidden = jnp.dot(lows[index], w_ref[...], preferred_element_type=jnp.float32)
+        out_ref[span] = hidden
+        gather_stats(stat_ref, hidden, (pl.program_id(0) == 0) if index == 0 else None)
 
 
 def norm_grad(upstream, normed, vec_ref):
@@ -965,7 +972,7 @@
     (out_hbm, heads_out, expand_out, spatial_out, reduce_out, vec_ref) = take(6)
     (two_buf, x_buf) = take(2)
     (side_ref, lane_ref, flow_ref, w_ref) = take(4)
-    heads_work, expand_work, spatial_work, reduce_work, stat_ref = take(5)
+    heads_work, expand_work, spatial_work, reduce_work, total_ref, stat_ref = take(6)
     pair_sems, whole_sems, flow_sems = take(3)
     exchange = Exchange(tasks, batch, *take(6))
     grid = Grid(batch)
@@ -1015,7 +1022,7 @@
         works.append((spatial_work.at[span], spatial_out.at[span], "tall"))
     for index in range(2):
         span = pl.ds(index * width // 2, width // 2)
-        works.append((reduce_work.at[span], reduce_out.at[span], "tall"))
+        works.append((reduce_work.at[span], total_ref.at[span], "tall"))
     reductions = []
     for work, out, kind in works:
         shape = heads_out.shape if kind == "owner" else None
@@ -1101,7 +1108,10 @@
 
     lax.fori_loop(0, spans, taps, 0)
     columns.start(0)
-    settle_stats(exchange, stat_ref, [vecone_ref], vec_ref, rows, rows * tasks * batch, False)
+    settle_stats(
+        exchange, stat_ref, [vecone_ref], vec_ref, rows, rows * tasks * batch, False,
+        (lambda: tick("xa"), lambda: tick("xb")),
+    )
     tick("xch")
 
     def inner(index, carry):
@@ -1127,6 +1137,9 @@
     lax.fori_loop(0, count, reduce, 0)
     keep.wait()
     tick("tail")
+    store = pltpu.make_async_copy(total_ref, reduce_out, whole_sems.at[0])
+    store.start()
+    store.wait()
 
 
 def back(flow, h_two, vec_two, h_one, vec_one, sides, cuts, w_spatial, flat_in, heads, expand, heads_shape, ident, tile):
@@ -1152,6 +1165,7 @@
         pltpu.VMEM(expand.shape, low),
         pltpu.VMEM((9 * mid, mid), low),
         pltpu.VMEM((width, mid), low),
+        pltpu.VMEM((width, mid), low),
         pltpu.VMEM((16, mid), full),
         pltpu.SemaphoreType.DMA((4, 2)),
         pltpu.SemaphoreType.DMA((5,)),
@@ -1276,7 +1290,7 @@
         (cots, lambda ref: ref.at[other(), pl.ds(quarter, quarter)], (quarter, half), "task"),
     ]
     h_three, q_two, vec_three, top_two, cot_two = widen(
-        h_two, vec_two, w_expand, (params(gain_three, bias_three), True, 2), sends, pixels
+        h_two, vec_two, w_expand, (params(gain_three, bias_three), True, 2), sends, min(rows, 2 * pixels)
     )
     out_mine, flow, normed, grad_heads, rest, out_peer, vec_three = crown(
         h_three, flat_in, threshold.reshape(rows, width), cots, (cot_one, cot_two), top_mine, (top_one, top_two), vec_three,

time: 289 us -> 287 us (level)
  no operation moved by 1% of the time
where the time goes in v4:
time: 287 us
  Pallas kernels  284 us (99%)
    pallas_call x5, Pallas kernels, tiled(): pl.pallas_call(run, grid=(rows // tile,), out_shape=out_shape, in_specs=i...  157 us
    pallas_call x1, Pallas kernels, back(): pl.pallas_call(functools.partial(back_kernel, rows, tasks, batch, tile),...  107 us
    pallas_call x1, Pallas kernels, finish(): pl.pallas_call(finish_kernel, grid=(steps,), out_shape=outs + [both] + su...  20.6 us

profile of v4, /device:TPU:0, one launch (start us, length us, event | category | flops | bytes accessed | tf_op | source)
XLA Modules:
  0.0 286.7 jit_solution(11485551910829156147)
XLA Ops:
  0.6 1.3 copy.26.refs_2_.refs_10_
  2.0 20.8 %squeeze.5 = (f32[2048,512]{1,0:T(8,128)}, f32[16,512]{1,0:T(8,128)}) custom-call(bf16[2048,2048]{1,0:T(8,128)(2,1)} %bitcast.22, bf16[2048,512]{1,0:T(8,128)(2,1)} %w_ref.1, f32[1,512]{1,0:T(1,128)} %bitcast.34, f32[1,512]{1,0:T(1,128)} %bitcast.35), custom_call_target="tpu_custom_call" | custom-call | tf_op jit(solution)/shard_map/squeeze/pallas_call | solution.py:821
  22.8 28.5 %mesh_forward.1 = (f32[2048,512]{1,0:T(8,128)}, bf16[1536,2048]{1,0:T(8,128)(2,1)}, f32[16,512]{1,0:T(8,128)}, bf16[1024,256]{1,0:T(8,128)(2,1)}, bf16[512,256]{1,0:T(8,128)(2,1)}) custom-call(f32[2048,512]{1,0:T(8,128)} %get-tuple-element.54.refs_0_.refs_2_, f32[16,512]{1,0:T(8,128)} %get-tuple-element.55.refs_1_.refs_9_, s32[8,2]{1,0:T(8,128)} %copy.26.refs_2_.refs_10_, ...), custom_call_target="tpu_custom_call" | custom-call | tf_op jit(solution)/shard_map/mesh_forward/pallas_call | solution.py:821
  51.3 22.4 %widen.1 = (f32[2048,2048]{1,0:T(8,128)}, bf16[512,2048]{1,0:T(8,128)(2,1)}, f32[16,2048]{1,0:T(8,128)}, bf16[1024,256]{1,0:T(8,128)(2,1)}, bf16[512,256]{1,0:T(8,128)(2,1)}) custom-call(f32[2048,512]{1,0:T(8,128)} %get-tuple-element.56.refs_0_.refs_3_.refs_1_, f32[16,512]{1,0:T(8,128)} %get-tuple-element.57.refs_1_.refs_4_.refs_7_, ...), custom_call_target="tpu_custom_call" | custom-call | tf_op jit(solution)/shard_map/widen/pallas_call | solution.py:821
  73.7 52.5 %crown.1 = (f32[2048,256]{1,0:T(8,128)}, bf16[2048,2048]{1,0:T(8,128)(2,1)}, bf16[2048,2048]{1,0:T(8,128)(2,1)}, bf16[2048,512]{1,0:T(8,128)(2,1)}, bf16[256,256...) custom-call(f32[2048,2048]{1,0:T(8,128)} %get-tuple-element.59.refs_0_, bf16[2048,2048]{1,0:T(8,128)(2,1)} %bitcast.23, ...), custom_call_target="tpu_custom_call" | custom-call | tf_op jit(solution)/shard_map/crown/pallas_call | solution.py:821
  126.2 32.5 %narrow.1 = (f32[2048,512]{1,0:T(8,128)}, bf16[512,2048]{1,0:T(8,128)(2,1)}, f32[16,512]{1,0:T(8,128)}, bf16[256,256]{1,0:T(8,128)(2,1)}, bf16[2,256,256]{2,1,0:T(8,128)(2,1)}) custom-call(bf16[2048,2048]{1,0:T(8,128)(2,1)} %get-tuple-element.64.refs_0_.up_ref, bf16[2048,2048]{1,0:T(8,128)(2,1)} %get-tuple-element.65.refs_1_, ...), custom_call_target="tpu_custom_call" | custom-call | tf_op jit(solution)/shard_map/narrow/pallas_call | solution.py:821
  158.7 107.2 %back.1 = (bf16[2048,512]{1,0:T(8,128)(2,1)}, bf16[2048,512]{1,0:T(8,128)(2,1)}, bf16[512,2048]{1,0:T(8,128)(2,1)}, bf16[4608,512]{1,0:T(8,128)(2,1)}, bf16[2048,512]{1,0:T(8,128)(2,1)}, /*index=5*/f32[16,512]{1,0:T(8,128)}) custom-call(f32[2048,512]{1,0:T(8,128)} %get-tuple-element.70.refs_0_, f32[2048,512]{1,0:T(8,128)} %get-tuple-element.56.refs_0_.refs_3_.refs_1_, ...), custom_call_target="tpu_custom_call" | custom-call | tf_op jit(solution)/shard_map/back/pallas_call | solution.py:1176
  265.9 20.6 %finish.1 = (bf16[2048,2048]{1,0:T(8,128)(2,1)}, f32[2048,256]{1,0:T(8,128)}, f32[512,2048]{1,0:T(8,128)}, f32[4608,512]{1,0:T(8,128)}, f32[2048,512]{1,0:T(8,12...) custom-call(bf16[2048,512]{1,0:T(8,128)(2,1)} %get-tuple-element.75., ...), custom_call_target="tpu_custom_call" | custom-call | tf_op jit(solution)/shard_map/finish/pallas_call | solution.py:1237

commit v5 on v4

--- a/solution.py
+++ b/solution.py
@@ -890,7 +890,7 @@
         def _():
             self.sum.stage(1)
 
-        @pl.when(step == self.last)
+        @pl.when(step == max(self.last - 2, 1))
         def _():
             self.sum.stage(2)
 
@@ -1298,7 +1298,7 @@
     )
     heads_shape = grad_heads.shape
     flow_two, grad_expand, vec_two, rest, grad_heads = narrow(
-        flow, normed, vec_three, h_two, vec_two, q_two, w_expand, grad_heads, rest, ([vec_two], False, 4), min(rows, 512)
+        flow, normed, vec_three, h_two, vec_two, q_two, w_expand, grad_heads, rest, ([vec_two], False, 4), pixels
     )
     dh_one, grad_heads, grad_expand, grad_spatial, grad_reduce, vec_one = back(
         flow_two, h_two, vec_two, h_one, vec_one, sides, cuts, w_spatial, flat_in, grad_heads, grad_expand, heads_shape, 5,

time: 287 us -> 286 us (level)
  no operation moved by 1% of the time
where the time goes in v5:
time: 286 us; the launch traced here: 285 us
  Pallas kernels  283 us (99%)
    pallas_call x5, Pallas kernels, tiled(): pl.pallas_call(run, grid=(rows // tile,), out_shape=out_shape, in_specs=i...  155 us
    pallas_call x1, Pallas kernels, back(): pl.pallas_call(functools.partial(back_kernel, rows, tasks, batch, tile),...  107 us
    pallas_call x1, Pallas kernels, finish(): pl.pallas_call(finish_kernel, grid=(steps,), out_shape=outs + [both] + su...  20.6 us

profile of v5, /device:TPU:0, one launch (start us, length us, event | category | flops | bytes accessed | tf_op | source)
XLA Modules:
  0.0 284.9 jit_solution(8443916755217104187)
XLA Ops:
  0.6 1.3 copy.26.refs_2_.refs_10_
  2.0 20.8 %squeeze.5 = (f32[2048,512]{1,0:T(8,128)}, f32[16,512]{1,0:T(8,128)}) custom-call(bf16[2048,2048]{1,0:T(8,128)(2,1)} %bitcast.22, bf16[2048,512]{1,0:T(8,128)(2,1)} %w_ref.1, f32[1,512]{1,0:T(1,128)} %bitcast.34, f32[1,512]{1,0:T(1,128)} %bitcast.35), custom_call_target="tpu_custom_call" | custom-call | tf_op jit(solution)/shard_map/squeeze/pallas_call | solution.py:821
  22.8 28.5 %mesh_forward.1 = (f32[2048,512]{1,0:T(8,128)}, bf16[1536,2048]{1,0:T(8,128)(2,1)}, f32[16,512]{1,0:T(8,128)}, bf16[1024,256]{1,0:T(8,128)(2,1)}, bf16[512,256]{1,0:T(8,128)(2,1)}) custom-call(f32[2048,512]{1,0:T(8,128)} %get-tuple-element.54.refs_0_.refs_2_, f32[16,512]{1,0:T(8,128)} %get-tuple-element.55.refs_1_.refs_9_, s32[8,2]{1,0:T(8,128)} %copy.26.refs_2_.refs_10_, ...), custom_call_target="tpu_custom_call" | custom-call | tf_op jit(solution)/shard_map/mesh_forward/pallas_call | solution.py:821
  51.3 22.4 %widen.1 = (f32[2048,2048]{1,0:T(8,128)}, bf16[512,2048]{1,0:T(8,128)(2,1)}, f32[16,2048]{1,0:T(8,128)}, bf16[1024,256]{1,0:T(8,128)(2,1)}, bf16[512,256]{1,0:T(8,128)(2,1)}) custom-call(f32[2048,512]{1,0:T(8,128)} %get-tuple-element.56.refs_0_.refs_3_.refs_1_, f32[16,512]{1,0:T(8,128)} %get-tuple-element.57.refs_1_.refs_4_.refs_7_, ...), custom_call_target="tpu_custom_call" | custom-call | tf_op jit(solution)/shard_map/widen/pallas_call | solution.py:821
  73.7 52.5 %crown.1 = (f32[2048,256]{1,0:T(8,128)}, bf16[2048,2048]{1,0:T(8,128)(2,1)}, bf16[2048,2048]{1,0:T(8,128)(2,1)}, bf16[2048,512]{1,0:T(8,128)(2,1)}, bf16[256,256...) custom-call(f32[2048,2048]{1,0:T(8,128)} %get-tuple-element.59.refs_0_, bf16[2048,2048]{1,0:T(8,128)(2,1)} %bitcast.23, ...), custom_call_target="tpu_custom_call" | custom-call | tf_op jit(solution)/shard_map/crown/pallas_call | solution.py:821
  126.2 30.6 %narrow.1 = (f32[2048,512]{1,0:T(8,128)}, bf16[512,2048]{1,0:T(8,128)(2,1)}, f32[16,512]{1,0:T(8,128)}, bf16[256,256]{1,0:T(8,128)(2,1)}, bf16[2,256,256]{2,1,0:T(8,128)(2,1)}) custom-call(bf16[2048,2048]{1,0:T(8,128)(2,1)} %get-tuple-element.64.refs_0_.up_ref, bf16[2048,2048]{1,0:T(8,128)(2,1)} %get-tuple-element.65.refs_1_, ...), custom_call_target="tpu_custom_call" | custom-call | tf_op jit(solution)/shard_map/narrow/pallas_call | solution.py:821
  156.9 107.3 %back.1 = (bf16[2048,512]{1,0:T(8,128)(2,1)}, bf16[2048,512]{1,0:T(8,128)(2,1)}, bf16[512,2048]{1,0:T(8,128)(2,1)}, bf16[4608,512]{1,0:T(8,128)(2,1)}, bf16[2048,512]{1,0:T(8,128)(2,1)}, /*index=5*/f32[16,512]{1,0:T(8,128)}) custom-call(f32[2048,512]{1,0:T(8,128)} %get-tuple-element.70.refs_0_, f32[2048,512]{1,0:T(8,128)} %get-tuple-element.56.refs_0_.refs_3_.refs_1_, ...), custom_call_target="tpu_custom_call" | custom-call | tf_op jit(solution)/shard_map/back/pallas_call | solution.py:1176
  264.1 20.6 %finish.1 = (bf16[2048,2048]{1,0:T(8,128)(2,1)}, f32[2048,256]{1,0:T(8,128)}, f32[512,2048]{1,0:T(8,128)}, f32[4608,512]{1,0:T(8,128)}, f32[2048,512]{1,0:T(8,12...) custom-call(bf16[2048,512]{1,0:T(8,128)(2,1)} %get-tuple-element.75., ...), custom_call_target="tpu_custom_call" | custom-call | tf_op jit(solution)/shard_map/finish/pallas_call | solution.py:1237
